TPU v7x, 256 devices: a whole 4x4x8 slice. The times are simulated.
256 devices in a mesh: grp: 8 (over x, core), rep: 32 (over z, y).
Axes of the slice: x: 4, y: 4, z: 8, core: 2. Of those that a mesh axis runs over, the one named last changes fastest.
Arguments:
- tokens: bfloat16 [131072, 1024], P(('grp', 'rep')), may hold values from -42 to 42
- owner: int32 [131072, 1], P(('grp', 'rep')), may hold values from 0 to 7; in each aligned block of 512 rows (0 to 511, 512 to 1023, ...) at most 128 rows name the same one
- list_local: int32 [131072], P(('grp', 'rep')), may hold values from 0 to 1023
- centroids: bfloat16 [262144, 1024], P(('grp', 'rep')), may hold values from -5 to 5
- rotation: bfloat16 [1024, 1024], replicated, may hold values from -0.1875 to 0.1875
- codebook: float32 [16, 64, 256], replicated, may hold values from -7 to 7
Outputs:
- new_codebook: float32 [16, 64, 256], replicated
- cross_cov: float32 [1024, 1024], P(('grp', 'rep'))
Inputs may be any that keep to these rules, and one draw needn't show every extreme that they name: Among the rows of one device at most 128 name the same owner, and some device has exactly 128 for some owner.
All inputs are finite; a program needn't handle non-finite values.
Results may differ from a plain program's by a relative error of at most 0.0048.
The roundings to bfloat16 on the way count: a program that leaves them out, or rounds other values in their place, can miss the bound.
Values may be sent and summed in bfloat16 or wider, within the bound.
No kernel may reach another device: no remote copies, remote signals or barrier semaphores. Data moves between devices by JAX's collectives and lax.ppermute only.
A program may use at most 64 MiB of HBM per device.

v0:
```python
import math

import jax
import jax.numpy as jnp
from jax import lax
from jax.sharding import Mesh
from jax.sharding import PartitionSpec as P

GRP = ("grp_0", "grp_1")
REP = ("rep_0", "rep_1")
GRP_REP = ("grp_0", "grp_1", "rep_0", "rep_1")


INV_TEMP = 0.2


def cut_along(value, dim, length):
    shape = value.shape
    pieces = value.reshape(*shape[:dim], length, shape[dim] // length, *shape[dim + 1 :])
    return jnp.moveaxis(pieces, dim, 0)


def sent_and_summed(value, axis, dim):
    pieces = cut_along(value, dim, lax.axis_size(axis))
    arrived = lax.all_to_all(pieces, axis, split_axis=0, concat_axis=0, tiled=True)
    return arrived.sum(axis=0)


def sum_by_axis(value, axes, dim):
    far, near = axes
    pieces = cut_along(value, dim, lax.axis_size(far))
    nearer = sent_and_summed(pieces, near, dim + 1)
    arrived = lax.all_to_all(nearer, far, split_axis=0, concat_axis=0, tiled=True)
    return arrived.sum(axis=0)


def rows_for(lines, length):
    spare = -lines.shape[0] % length
    if not spare:
        return lines
    return jnp.concatenate([lines, jnp.zeros((spare, *lines.shape[1:]), lines.dtype)])


def sent_to_all(value, axis):
    copies = jnp.broadcast_to(value, (lax.axis_size(axis), *value.shape))
    return lax.all_to_all(copies, axis, split_axis=0, concat_axis=0, tiled=True)


def in_order(pieces, dim):
    shape = list(pieces.shape[1:])
    shape[dim] *= pieces.shape[0]
    return jnp.moveaxis(pieces, 0, dim).reshape(shape)


def whole_of(value, axes, dim):
    far, near = axes
    pieces = sent_to_all(sent_to_all(value, far), near)
    return in_order(pieces.swapaxes(0, 1).reshape(-1, *value.shape), dim)


def total_of(value, axes):
    padded = rows_for(value, lax.axis_size(axes[0]) * lax.axis_size(axes[1]))
    whole = whole_of(sum_by_axis(padded, axes, 0), axes, 0)
    return lax.slice_in_dim(whole, 0, len(value)).reshape(value.shape)


def in_one(arrays, axis):
    ends = [0]
    for a in arrays:
        ends.append(ends[-1] + a.size)
    subtotal = total_of(jnp.concatenate([a.ravel() for a in arrays]), axis)
    return tuple((subtotal[b:e].reshape(a.shape) for a, b, e in zip(arrays, ends, ends[1:])))


def code_stats(residual, weight, rotation, codebook):
    highest = lax.Precision.HIGHEST
    count_rows = residual.shape[0]
    feat_width = residual.shape[1]
    subs_count = codebook.shape[0]
    sub_width = codebook.shape[1]
    block = min(512, count_rows)
    turns = count_rows // block
    norms = jnp.sum(codebook * codebook, axis=1)

    def one_block(carry, inputs):
        num_acc, cnt_acc = carry
        piece, row_mask = inputs
        rotated = jnp.dot(piece, rotation, preferred_element_type=jnp.float32).reshape(
            block, subs_count, sub_width
        )
        logits = (
            2.0 * jnp.einsum("smj,mjk->smk", rotated, codebook, precision=highest) - norms[None]
        ) * INV_TEMP
        prob = jax.nn.softmax(logits, axis=-1) * row_mask[:, None, None]
        num = jnp.einsum("smk,smj->mjk", prob, rotated, precision=highest)
        cnt = jnp.sum(prob, axis=0)
        rebuilt = (
            jnp.einsum("smk,mjk->smj", prob, codebook, precision=highest)
            .reshape(block, feat_width)
            .astype(jnp.bfloat16)
        )
        return ((num_acc + num, cnt_acc + cnt), rebuilt)

    start = (
        jnp.zeros(codebook.shape, jnp.float32),
        jnp.zeros((subs_count, codebook.shape[2]), jnp.float32),
    )
    totals, rebuilt = lax.scan(
        one_block, start, (residual.reshape(turns, block, feat_width), weight.reshape(turns, block))
    )
    return (totals[0], totals[1], rebuilt.reshape(count_rows, feat_width))


def local(tokens, owner, list_local, centroids, rotation, codebook):
    groups = lax.axis_size(GRP)
    devices = groups * lax.axis_size(REP)
    row_dev = tokens.shape[0]
    feat_width = tokens.shape[1]
    slot_count = 2 * row_dev // groups
    target = owner[:, 0]
    onehot = (target[:, None] == jnp.arange(groups, dtype=jnp.int32)[None, :]).astype(jnp.int32)
    before = jnp.cumsum(onehot, axis=0) - onehot
    position = jnp.sum(before * onehot, axis=1)
    slot_index = target * slot_count + position
    send_ids = (
        jnp.full((groups * slot_count,), -1, jnp.int32)
        .at[slot_index]
        .set(list_local)
        .reshape(groups, slot_count)
    )
    send_rows = (
        jnp.zeros((groups * slot_count, feat_width), jnp.bfloat16)
        .at[slot_index]
        .set(tokens)
        .reshape(groups, slot_count, feat_width)
    )
    got_rows, got_ids = (
        lax.all_to_all(send_rows, GRP, split_axis=0, concat_axis=0, tiled=True),
        lax.all_to_all(send_ids, GRP, split_axis=0, concat_axis=0, tiled=True),
    )
    got_rows = got_rows.reshape(groups * slot_count, feat_width)
    got_ids = got_ids.reshape(groups * slot_count)
    is_valid = got_ids >= 0
    centre_rows = centroids[jnp.maximum(got_ids, 0)]
    residual = jnp.where(
        is_valid[:, None], got_rows.astype(jnp.float32) - centre_rows.astype(jnp.float32), 0.0
    ).astype(jnp.bfloat16)
    weight = is_valid.astype(jnp.float32)
    num, cnt, rebuilt = code_stats(residual, weight, rotation, codebook)
    columns = lax.slice_in_dim(residual, 0, feat_width // devices * lax.axis_size(GRP_REP), axis=1)
    cross_part = sum_by_axis(
        lax.dot_general(
            columns, rebuilt, (((0,), (0,)), ((), ())), preferred_element_type=jnp.float32
        ),
        (("grp_0", "grp_1", "rep_0"), "rep_1"),
        0,
    )
    cross_cov = cross_part * (1.0 / math.sqrt(row_dev * devices))
    num_total, cnt_total = in_one((num, cnt), (("grp_0", "grp_1", "rep_0"), "rep_1"))
    new_codebook = (num_total + codebook) / (cnt_total[:, None, :] + 1.0)
    return (new_codebook, cross_cov)


def solution(mesh):
    finer = Mesh(mesh.devices.reshape(4, 2, 8, 4), ("grp_0", "grp_1", "rep_0", "rep_1"))
    in_specs = (P(GRP_REP, None), P(GRP_REP, None), P(GRP_REP), P(GRP_REP, None), P(), P())
    out_specs = (P(), P(GRP_REP, None))
    return jax.shard_map(local, mesh=finer, in_specs=in_specs, out_specs=out_specs, check_vma=False)
```

profile of v0, /device:TPU:1, one launch (start us, length us, event | category | flops | bytes accessed | tf_op | source)
XLA Modules:
  0.0 316.9 jit_solution(2704233635498491634)
XLA Ops:
  4.3 3.2 scatter_custom_fusion
  7.5 6.5 %all-to-all-start = ((s32[8,1,128]{2,1,0:T(1,128)}), s32[8,1,128]{2,1,0:T(1,128)S(1)}, u32[]{:S(2)}, u32[]{:S(2)}) async-start(s32[8,1,128]{2,1,0:T(1,128)} %bitcast.6), calls=%async_computation | async-start | bytes 8192 | tf_op jit(solution)/shard_map/all_to_all | solution.py:139
  13.9 4.8 %scatter_custom_fusion.1 = bf16[1024,1024]{1,0:T(8,128)(2,1)} fusion(s32[512]{0:T(512)S(1)} %bitcast.127, bf16[512,1024]{1,0:T(8,128)(2,1)} %param.8, bf16[]{:T(256)} %constant.24.clone.1), kind=kCustom, calls=%fused_computation.36 | custom fusion | bytes 2097664 | tf_op jit(solution)/shard_map/scatter | solution.py:134
  18.8 4.8 %all-to-all-start.1 = ((bf16[8,128,1024]{2,1,0:T(8,128)(2,1)}), bf16[8,128,1024]{2,1,0:T(8,128)(2,1)}, u32[]{:S(2)}, u32[]{:S(2)}) async-start(bf16[8,128,1024]{2,1,0:T(8,128)(2,1)} %bitcast.107), calls=%async_computation.1 | async-start | bytes 4194304 | tf_op jit(solution)/shard_map/all_to_all | solution.py:138
  23.6 4.0 %copy.39 = bf16[1024,1024]{0,1:T(8,128)(2,1)} copy(bf16[1024,1024]{1,0:T(8,128)(2,1)} %param.12) | data formatting | bytes 4194304
  27.8 5.4 %gather_fusion = bf16[1024,1024]{1,0:T(8,128)(2,1)} fusion(bf16[1024,1024]{1,0:T(8,128)(2,1)S(1)} %copy-done, s32[1024]{0:T(1024)S(1)} %bitcast_clamp_fusion), kind=kCustom, calls=%fused_computation | custom fusion | bytes 4198400 | tf_op jit(solution)/shard_map/gather | solution.py:144
  33.2 16.8 %all-to-all-done.1 = bf16[8,128,1024]{2,1,0:T(8,128)(2,1)} async-done(((bf16[8,128,1024]{2,1,0:T(8,128)(2,1)}), bf16[8,128,1024]{2,1,0:T(8,128)(2,1)}, u32[]{:S(2)}, u32[]{:S(2)}) %all-to-all-start.1) | async-done | bytes 2097184 | tf_op jit(solution)/shard_map/all_to_all | solution.py:138
  50.0 2.0 convert_element_type.66
  52.1 1.9 fusion.18
  54.0 79.7 %while.15 = (s32[]{:T(128)}, f32[16,64,256]{2,1,0:T(8,128)}, f32[16,256]{1,0:T(8,128)S(1)}, bf16[2,512,1024]{2,1,0:T(8,128)(2,1)}, bf16[2,512,1024]{2,1,0:T(8,12...) while((s32[]{:T(128)}, f32[16,64,256]{2,1,0:T(8,128)}, ...), condition=%wide.region_10.11_spmd.clone, body=%wide.region_6.10_spmd.clone.sunk | while | flops 5938089984 | bytes 77818048 | solution.py:108
  68.7 3.2 %fusion.52 = f32[512,16,64]{0,2,1:T(8,128)S(1)} fusion(bf16[16,64,1024]{2,1,0:T(8,128)(2,1)} %bitcast.112, bf16[2,512,1024]{2,1,0:T(8,128)(2,1)} %get-tuple-element.234, s32[]{:T(128)S(6)} %copy.66), kind=kOutput, calls=%fused_computation.15.clone.1 | convolution fusion | flops 1073741824 | bytes 5242884 | tf_op jit(solution)/shard_map/while/body/eval_jaxpr/dot_general | solution.py:88
  71.9 6.8 %fusion.53 = f32[16,512,256]{1,2,0:T(8,128)S(1)} fusion(f32[512,16,64]{0,2,1:T(8,128)S(1)} %fusion.52, f32[16,64,256]{2,1,0:T(8,128)S(1)} %get-tuple-element.236), kind=kOutput, calls=%fused_computation.54.clone.1 | convolution fusion | flops 1610612736 | bytes 11534336 | tf_op jit(solution)/shard_map/while/body/eval_jaxpr/smj,mjk->smk/dot_general | solution.py:92
  78.8 4.5 %fusion.54 = (f32[512,16]{0,1:T(8,128)S(1)}, f32[512,16,256]{0,2,1:T(8,128)S(1)}) fusion(f32[16,512,256]{1,2,0:T(8,128)S(1)} %fusion.53, f32[16,256]{1,0:T(8,128)S(1)} %get-tuple-element.237), kind=kOutput, calls=%fused_computation.53.clone.1 | output fusion | flops 16777472 | bytes 16826368 | tf_op jit(solution)/shard_map/while/body/eval_jaxpr/sub | solution.py:94
  83.3 8.4 %convolution_add_fusion.2 = f32[16,64,256]{2,1,0:T(8,128)S(1)} fusion(f32[512,16,64]{0,2,1:T(8,128)S(1)} %fusion.52, f32[16,64,256]{2,1,0:T(8,128)S(1)} %copy-done.6, pred[]{:T(512)S(6)} %compare.3, f32[512,16,256]{0,2,1:T(8,128)S(1)} %get-tuple-element.206, f32[512]{0:T(512)S(1)} %bitcast.116, f32[512,16]{0,1:T(8,128)S(1)} %get-tuple-element.207), kind=kOutput, calls=%fused_computation.14.clone.1 | convolution fusion | flops 1615331328 | bytes 12617729 | tf_op jit(solution)/shard_map/while/body/eval_jaxpr/smk,smj->mjk/dot_general | solution.py:95
  93.6 6.0 %convolution_convert_fusion.2 = bf16[16,512,64]{1,2,0:T(8,128)(2,1)S(1)} fusion(f32[16,64,256]{2,1,0:T(8,128)S(1)} %get-tuple-element.236, f32[512,16,256]{0,2,1:T(8,128)S(1)} %get-tuple-element.206, f32[512]{0:T(512)S(1)} %bitcast.118, f32[512,16]{0,1:T(8,128)S(1)} %get-tuple-element.207), kind=kOutput, calls=%fused_computation.13.clone.1 | convolution fusion | flops 1615331328 | bytes 10520576 | tf_op jit(solution)/shard_map/while/body/eval_jaxpr/smk,mjk->smj/dot_general | solution.py:98
  100.1 1.1 constant_dynamic-update-slice_fusion.2
  101.3 3.2 %fusion.52 = f32[512,16,64]{0,2,1:T(8,128)S(1)} fusion(bf16[16,64,1024]{2,1,0:T(8,128)(2,1)} %bitcast.112, bf16[2,512,1024]{2,1,0:T(8,128)(2,1)} %get-tuple-element.234, s32[]{:T(128)S(6)} %copy.66), kind=kOutput, calls=%fused_computation.15.clone.1 | convolution fusion | flops 1073741824 | bytes 5242884 | tf_op jit(solution)/shard_map/while/body/eval_jaxpr/dot_general | solution.py:88
  104.5 6.8 %fusion.53 = f32[16,512,256]{1,2,0:T(8,128)S(1)} fusion(f32[512,16,64]{0,2,1:T(8,128)S(1)} %fusion.52, f32[16,64,256]{2,1,0:T(8,128)S(1)} %get-tuple-element.236), kind=kOutput, calls=%fused_computation.54.clone.1 | convolution fusion | flops 1610612736 | bytes 11534336 | tf_op jit(solution)/shard_map/while/body/eval_jaxpr/smj,mjk->smk/dot_general | solution.py:92
  111.3 4.5 %fusion.54 = (f32[512,16]{0,1:T(8,128)S(1)}, f32[512,16,256]{0,2,1:T(8,128)S(1)}) fusion(f32[16,512,256]{1,2,0:T(8,128)S(1)} %fusion.53, f32[16,256]{1,0:T(8,128)S(1)} %get-tuple-element.237), kind=kOutput, calls=%fused_computation.53.clone.1 | output fusion | flops 16777472 | bytes 16826368 | tf_op jit(solution)/shard_map/while/body/eval_jaxpr/sub | solution.py:94
  115.8 8.4 %convolution_add_fusion.2 = f32[16,64,256]{2,1,0:T(8,128)S(1)} fusion(f32[512,16,64]{0,2,1:T(8,128)S(1)} %fusion.52, f32[16,64,256]{2,1,0:T(8,128)S(1)} %copy-done.6, pred[]{:T(512)S(6)} %compare.3, f32[512,16,256]{0,2,1:T(8,128)S(1)} %get-tuple-element.206, f32[512]{0:T(512)S(1)} %bitcast.116, f32[512,16]{0,1:T(8,128)S(1)} %get-tuple-element.207), kind=kOutput, calls=%fused_computation.14.clone.1 | convolution fusion | flops 1615331328 | bytes 12617729 | tf_op jit(solution)/shard_map/while/body/eval_jaxpr/smk,smj->mjk/dot_general | solution.py:95
  126.1 6.0 %convolution_convert_fusion.2 = bf16[16,512,64]{1,2,0:T(8,128)(2,1)S(1)} fusion(f32[16,64,256]{2,1,0:T(8,128)S(1)} %get-tuple-element.236, f32[512,16,256]{0,2,1:T(8,128)S(1)} %get-tuple-element.206, f32[512]{0:T(512)S(1)} %bitcast.118, f32[512,16]{0,1:T(8,128)S(1)} %get-tuple-element.207), kind=kOutput, calls=%fused_computation.13.clone.1 | convolution fusion | flops 1615331328 | bytes 10520576 | tf_op jit(solution)/shard_map/while/body/eval_jaxpr/smk,mjk->smj/dot_general | solution.py:98
  133.7 1.8 copy.53
  136.5 2.1 reshape_reshape.7
  138.8 18.9 %all_to_all.52 = f32[4,64,1040]{2,1,0:T(8,128)} all-to-all(f32[4,64,1040]{2,1,0:T(8,128)S(1)} %copy.40), channel_id=1, replica_groups=mesh['grp_0'=4,'grp_1'=2,'rep_0'=8,'rep_1'=4] {'rep_1'}, dimensions={0} | all-to-all | bytes 2129920 | tf_op jit(solution)/shard_map/all_to_all | solution.py:25
  157.7 1.4 reduce_sum.77
  160.0 11.7 %all-to-all-start.3 = ((f32[64,1,1040]{2,1,0:T(1,128)}), f32[64,1,1040]{2,1,0:T(1,128)S(1)}, u32[]{:S(2)}, u32[]{:S(2)}) async-start(f32[64,1,1040]{2,1,0:T(1,128)} %all_to_all.37), calls=%async_computation.3 | async-start | bytes 589824 | tf_op jit(solution)/shard_map/all_to_all | solution.py:33
  171.8 3.5 %fusion.16 = bf16[1024,1024]{1,0:T(8,128)(2,1)} fusion(pred[1024]{0:T(1024)(128)(4,1)S(1)} %fusion.35, bf16[1024,1024]{1,0:T(8,128)(2,1)S(1)} %copy-done.4, bf16[8,128,1024]{2,1,0:T(8,128)(2,1)} %all-to-all-done.1), kind=kLoop, calls=%fused_computation.27 | loop fusion | flops 5242880 | bytes 6292480 | tf_op jit(solution)/shard_map/convert_element_type | solution.py:147
  175.3 2.9 copy.43
  178.2 2.2 dot_general.24
  180.4 4.0 %all-to-all-done.3 = f32[64,1,1040]{2,1,0:T(1,128)S(1)} async-done(((f32[64,1,1040]{2,1,0:T(1,128)}), f32[64,1,1040]{2,1,0:T(1,128)S(1)}, u32[]{:S(2)}, u32[]{:S(2)}) %all-to-all-start.3) | async-done | bytes 266272 | tf_op jit(solution)/shard_map/all_to_all | solution.py:33
  185.4 6.3 %all-to-all-start.4 = ((f32[64,1,1040]{2,1,0:T(1,128)}), f32[64,1,1040]{2,1,0:T(1,128)S(1)}, u32[]{:S(2)}, u32[]{:S(2)}) async-start(f32[64,1,1040]{2,1,0:T(1,128)} %broadcast_in_dim.55), calls=%async_computation.4 | async-start | bytes 589824 | tf_op jit(solution)/shard_map/all_to_all | solution.py:46
  191.8 6.9 %convolution_bitcast_fusion = f32[4,64,4,1024]{3,1,2,0:T(8,128)} fusion(bf16[1024,1024,1,1]{1,0,3,2:T(8,128)(2,1)} %bitcast.128, bf16[64,4,4,1024]{3,2,1,0:T(4,128)(2,1)} %dot_general.24), kind=kOutput, calls=%fused_computation.31 | convolution fusion | flops 2147483648 | bytes 8388608 | tf_op jit(solution)/shard_map/dot_general | solution.py:152
  198.7 5.7 %all-to-all-done.4 = f32[64,1,1040]{2,1,0:T(1,128)S(1)} async-done(((f32[64,1,1040]{2,1,0:T(1,128)}), f32[64,1,1040]{2,1,0:T(1,128)S(1)}, u32[]{:S(2)}, u32[]{:S(2)}) %all-to-all-start.4) | async-done | bytes 266272 | tf_op jit(solution)/shard_map/all_to_all | solution.py:46
  204.4 4.8 %all-to-all-start.6 = ((f32[4,64,4,1024]{3,1,2,0:T(8,128)}), f32[4,64,4,1024]{3,1,2,0:T(8,128)}, u32[]{:S(2)}, u32[]{:S(2)}) async-start(f32[4,64,4,1024]{3,1,2,0:T(8,128)} %convolution_bitcast_fusion), calls=%async_computation.6 | async-start | bytes 8388608 | tf_op jit(solution)/shard_map/all_to_all | solution.py:25
  209.3 47.5 %all-to-all-done.6 = f32[4,64,4,1024]{3,1,2,0:T(8,128)} async-done(((f32[4,64,4,1024]{3,1,2,0:T(8,128)}), f32[4,64,4,1024]{3,1,2,0:T(8,128)}, u32[]{:S(2)}, u32[]{:S(2)}) %all-to-all-start.6) | async-done | bytes 4194336 | tf_op jit(solution)/shard_map/all_to_all | solution.py:25
  257.9 3.5 %all-to-all-start.5 = ((f32[4,64,1040]{2,1,0:T(8,128)}), f32[4,64,1040]{2,1,0:T(8,128)S(1)}, u32[]{:S(2)}, u32[]{:S(2)}) async-start(f32[4,64,1040]{2,1,0:T(8,128)} %broadcast_in_dim.56), calls=%async_computation.5 | async-start | bytes 2359296 | tf_op jit(solution)/shard_map/all_to_all | solution.py:46
  261.4 3.7 %reduce_sum.79 = f32[64,4,1024]{2,0,1:T(8,128)} reduce(f32[4,64,4,1024]{3,1,2,0:T(8,128)} %all-to-all-done.6, f32[]{:T(128)} %constant.8.clone.1), dimensions={0}, to_apply=%region_13.14 | reduce | flops 786432 | bytes 5242884 | tf_op jit(solution)/shard_map/reduce_sum | solution.py:26
  265.1 2.9 copy.46
  268.0 7.6 %all-to-all-done.5 = f32[4,64,1040]{2,1,0:T(8,128)S(1)} async-done(((f32[4,64,1040]{2,1,0:T(8,128)}), f32[4,64,1040]{2,1,0:T(8,128)S(1)}, u32[]{:S(2)}, u32[]{:S(2)}) %all-to-all-start.5) | async-done | bytes 1064992 | tf_op jit(solution)/shard_map/all_to_all | solution.py:46
  275.7 10.8 %all-to-all-start.7 = ((f32[64,4,1024]{2,1,0:T(4,128)}), f32[64,4,1024]{2,1,0:T(4,128)}, u32[]{:S(2)}, u32[]{:S(2)}) async-start(f32[64,4,1024]{2,1,0:T(4,128)} %copy.46), calls=%async_computation.7 | async-start | bytes 2097152 | tf_op jit(solution)/shard_map/all_to_all | solution.py:33
  286.5 2.0 copy.41
  288.6 2.0 slice.18
  290.6 1.9 reshape_reshape.8
  292.5 1.2 slice-done
  293.7 1.3 reshape.118
  295.8 2.4 add_divide_fusion
  298.2 16.2 %all-to-all-done.7 = f32[64,4,1024]{2,1,0:T(4,128)} async-done(((f32[64,4,1024]{2,1,0:T(4,128)}), f32[64,4,1024]{2,1,0:T(4,128)}, u32[]{:S(2)}, u32[]{:S(2)}) %all-to-all-start.7) | async-done | bytes 1048608 | tf_op jit(solution)/shard_map/all_to_all | solution.py:33
  314.4 1.4 reduce_sum.80
  (61 shorter events, 15.5 us)
Async XLA Ops:
  0.6 27.2 %copy-start = (bf16[1024,1024]{1,0:T(8,128)(2,1)S(1)}, bf16[1024,1024]{1,0:T(8,128)(2,1)}, u32[]{:S(2)}) copy-start(bf16[1024,1024]{1,0:T(8,128)(2,1)} %param.11) | copy-start | bytes 6291460
  7.5 11.3 %all-to-all-start = ((s32[8,1,128]{2,1,0:T(1,128)}), s32[8,1,128]{2,1,0:T(1,128)S(1)}, u32[]{:S(2)}, u32[]{:S(2)}) async-start(s32[8,1,128]{2,1,0:T(1,128)} %bitcast.6), calls=%async_computation | async-start | bytes 8192 | tf_op jit(solution)/shard_map/all_to_all | solution.py:139
  18.8 9.0 %copy-start.8 = (s32[8,1,128]{2,1,0:T(1,128)}, s32[8,1,128]{2,1,0:T(1,128)S(1)}, u32[]{:S(2)}) copy-start(s32[8,1,128]{2,1,0:T(1,128)S(1)} %all-to-all-done) | copy-start | bytes 12292
  18.8 31.3 %all-to-all-start.1 = ((bf16[8,128,1024]{2,1,0:T(8,128)(2,1)}), bf16[8,128,1024]{2,1,0:T(8,128)(2,1)}, u32[]{:S(2)}, u32[]{:S(2)}) async-start(bf16[8,128,1024]{2,1,0:T(8,128)(2,1)} %bitcast.107), calls=%async_computation.1 | async-start | bytes 4194304 | tf_op jit(solution)/shard_map/all_to_all | solution.py:138
  23.6 4.1 %copy-start.2 = (f32[16,64,256]{2,1,0:T(8,128)S(1)}, f32[16,64,256]{2,1,0:T(8,128)}, u32[]{:S(2)}) copy-start(f32[16,64,256]{2,1,0:T(8,128)} %param.13) | copy-start | bytes 3145732
  33.2 18.9 %copy-start.3 = (bf16[1024,1024]{1,0:T(8,128)(2,1)S(1)}, bf16[1024,1024]{1,0:T(8,128)(2,1)}, u32[]{:S(2)}) copy-start(bf16[1024,1024]{1,0:T(8,128)(2,1)} %gather_fusion) | copy-start | bytes 6291460
  78.7 4.5 %copy-start.6 = (f32[16,64,256]{2,1,0:T(8,128)S(1)}, f32[16,64,256]{2,1,0:T(8,128)}, u32[]{:S(2)}) copy-start(f32[16,64,256]{2,1,0:T(8,128)} %get-tuple-element.220) | copy-start | bytes 3145732 | tf_op jit(solution)/shard_map/while
  91.7 1.0 copy-start.7
  111.3 4.5 %copy-start.6 = (f32[16,64,256]{2,1,0:T(8,128)S(1)}, f32[16,64,256]{2,1,0:T(8,128)}, u32[]{:S(2)}) copy-start(f32[16,64,256]{2,1,0:T(8,128)} %get-tuple-element.220) | copy-start | bytes 3145732 | tf_op jit(solution)/shard_map/while
  124.2 1.0 copy-start.7
  138.8 33.0 %copy-start.9 = (s32[8,1,128]{2,1,0:T(1,128)S(1)}, s32[8,1,128]{2,1,0:T(1,128)}, u32[]{:S(2)}) copy-start(s32[8,1,128]{2,1,0:T(1,128)} %copy-done.8) | copy-start | bytes 12292
  138.8 33.0 %copy-start.4 = (bf16[1024,1024]{1,0:T(8,128)(2,1)S(1)}, bf16[1024,1024]{1,0:T(8,128)(2,1)}, u32[]{:S(2)}) copy-start(bf16[1024,1024]{1,0:T(8,128)(2,1)} %gather_fusion) | copy-start | bytes 6291460
  160.0 24.4 %all-to-all-start.3 = ((f32[64,1,1040]{2,1,0:T(1,128)}), f32[64,1,1040]{2,1,0:T(1,128)S(1)}, u32[]{:S(2)}, u32[]{:S(2)}) async-start(f32[64,1,1040]{2,1,0:T(1,128)} %all_to_all.37), calls=%async_computation.3 | async-start | bytes 589824 | tf_op jit(solution)/shard_map/all_to_all | solution.py:33
  185.4 19.0 %all-to-all-start.4 = ((f32[64,1,1040]{2,1,0:T(1,128)}), f32[64,1,1040]{2,1,0:T(1,128)S(1)}, u32[]{:S(2)}, u32[]{:S(2)}) async-start(f32[64,1,1040]{2,1,0:T(1,128)} %broadcast_in_dim.55), calls=%async_computation.4 | async-start | bytes 589824 | tf_op jit(solution)/shard_map/all_to_all | solution.py:46
  204.4 52.4 %all-to-all-start.6 = ((f32[4,64,4,1024]{3,1,2,0:T(8,128)}), f32[4,64,4,1024]{3,1,2,0:T(8,128)}, u32[]{:S(2)}, u32[]{:S(2)}) async-start(f32[4,64,4,1024]{3,1,2,0:T(8,128)} %convolution_bitcast_fusion), calls=%async_computation.6 | async-start | bytes 8388608 | tf_op jit(solution)/shard_map/all_to_all | solution.py:25
  257.9 17.8 %all-to-all-start.5 = ((f32[4,64,1040]{2,1,0:T(8,128)}), f32[4,64,1040]{2,1,0:T(8,128)S(1)}, u32[]{:S(2)}, u32[]{:S(2)}) async-start(f32[4,64,1040]{2,1,0:T(8,128)} %broadcast_in_dim.56), calls=%async_computation.5 | async-start | bytes 2359296 | tf_op jit(solution)/shard_map/all_to_all | solution.py:46
  275.7 10.9 %copy-start.5 = (f32[4,64,1040]{2,1,0:T(8,128)}, f32[4,64,1040]{2,1,0:T(8,128)S(1)}, u32[]{:S(2)}) copy-start(f32[4,64,1040]{2,1,0:T(8,128)S(1)} %all-to-all-done.5) | copy-start | bytes 3194884
  275.7 38.7 %all-to-all-start.7 = ((f32[64,4,1024]{2,1,0:T(4,128)}), f32[64,4,1024]{2,1,0:T(4,128)}, u32[]{:S(2)}, u32[]{:S(2)}) async-start(f32[64,4,1024]{2,1,0:T(4,128)} %copy.46), calls=%async_computation.7 | async-start | bytes 2097152 | tf_op jit(solution)/shard_map/all_to_all | solution.py:33
  292.5 1.2 slice-start
  295.0 21.4 %copy-start.1 = (bf16[1024,1024]{1,0:T(8,128)(2,1)S(1)}, bf16[1024,1024]{1,0:T(8,128)(2,1)}, u32[]{:S(2)}) copy-start(bf16[1024,1024]{1,0:T(8,128)(2,1)} %param.11) | copy-start | bytes 6291460
where the time goes:
time: 323 us; the launch traced here: 317 us
  waiting for transfers between devices  97.9 us (30%)
  matrix products  55.7 us (17%)
  starting transfers between devices  48.5 us (15%)
  local copies, waits for them, and re-layouts  46.2 us (14%)
  other arithmetic  33.5 us (10%)
  blocking collectives  18.9 us (6%)
  loops' own time  14.8 us (5%)
    all_to_all x1, waiting for transfers between devices, sent_and_summed(): lax.all_to_all(pieces, axis, split_axis=0, concat_axis=0, tiled=True)  47.5 us
    all_to_all x2, starting transfers between devices, sum_by_axis(): lax.all_to_all(nearer, far, split_axis=0, concat_axis=0, tiled=True)  22.6 us
    all_to_all x2, waiting for transfers between devices, sum_by_axis(): lax.all_to_all(nearer, far, split_axis=0, concat_axis=0, tiled=True)  20.2 us
    all_to_all x1, blocking collectives, sent_and_summed(): lax.all_to_all(pieces, axis, split_axis=0, concat_axis=0, tiled=True)  18.9 us
    dot_general x2, matrix products, one_block(): num = jnp.einsum('smk,smj->mjk', prob, rotated, precision=highest)  16.8 us
    all_to_all x1, waiting for transfers between devices, local(): lax.all_to_all(send_rows, GRP, split_axis=0, concat_axis=0, tiled=True)  16.8 us
    another operation x1, loops' own time, code_stats(): lax.scan(one_block, start, (residual.reshape(turns, block, feat_width), w...  14.8 us
    dot_general x2, matrix products, one_block(): jnp.einsum('smj,mjk->smk', rotated, codebook, precision=highest)  13.6 us
  transfers between devices with their start and end apart: 7, of which 6 were waited for; matrix products, arithmetic and copies ran while one was open for 15% of the time, Pallas kernels for 0%

commit v1 on v0

v1 whole, which is shorter than its diff:
```python
import math

import jax
import jax.numpy as jnp
from jax import lax
from jax.experimental import pallas as pl
from jax.experimental.pallas import tpu as pltpu
from jax.sharding import Mesh
from jax.sharding import PartitionSpec as P

ALL = ("x", "c", "z", "y")
GRP = ("x", "c")
OWNERS = 8
CAP = 128
LISTS = 1024
ROWS = 512
D = 1024
M = 16
DSUB = 64
K = 256
WIDE = D + 2 * K
INV_TEMP = 0.2
F32 = jnp.float32
BF16 = jnp.bfloat16


def dot(a, b, ca=1, cb=0):
    return lax.dot_general(a, b, (((ca,), (cb,)), ((), ())), preferred_element_type=F32)


def iota(shape, dim):
    return lax.broadcasted_iota(jnp.int32, shape, dim)


def one_hot(hit):
    return jnp.where(hit, 1.0, 0.0).astype(BF16)


def slots_kernel(owner_ref, lists_ref, slot_ref, ids_ref):
    owner = owner_ref[...]
    mine = owner == iota((ROWS, 128), 1)
    earlier = one_hot(iota((ROWS, ROWS), 0) > iota((ROWS, ROWS), 1))
    before = dot(earlier, one_hot(mine))
    position = jnp.sum(jnp.where(mine, before, 0.0), axis=1, keepdims=True)
    slot = owner * CAP + position.astype(jnp.int32)
    slot_ref[...] = slot
    lists = lists_ref[...]
    row = iota((8, ROWS), 0)
    parts = jnp.where(row == 0, lists >> 5, jnp.where(row == 1, lists & 31, 1))
    sent = dot(parts.astype(F32).astype(BF16), one_hot(slot == iota((ROWS, OWNERS * CAP), 1)))
    ids = sent[0:1] * 32.0 + sent[1:2] + sent[2:3] - 1.0
    for o in range(OWNERS):
        ids_ref[o : o + 1, :] = ids[:, o * CAP : (o + 1) * CAP].astype(jnp.int32)


def centres_kernel(ids_ref, centroids_ref, out_ref):
    ids = ids_ref[...].astype(F32).T.astype(jnp.int32)
    table = centroids_ref[...]
    for s in range(OWNERS):
        pick = one_hot(ids[:, s : s + 1] == iota((CAP, LISTS), 1))
        out_ref[s] = dot(pick, table).astype(BF16)


def codes_kernel(book_ref, stack_ref, turned_ref, norm_ref):
    for i in range(4):
        book = book_ref[i]
        high = book.astype(BF16)
        low = (book - high.astype(F32)).astype(BF16)
        stack_ref[i] = jnp.concatenate([high, low, high, low], axis=0)
        turned = jnp.concatenate([high.astype(F32), low.astype(F32)], axis=0).T
        turned_ref[i] = turned.astype(BF16)
        norm_ref[i] = INV_TEMP * jnp.sum(book * book, axis=0, keepdims=True)


def stats_kernel(
    tokens_ref, slot_ref, got_ref, rotation_ref, stack_ref, turned_ref, norm_ref,
    out_ref, res_ref, turned_res_ref,
):
    step = pl.program_id(0)

    @pl.when(step == 0)
    def _():
        pick = one_hot(slot_ref[...] == iota((ROWS, OWNERS * CAP), 1))
        centres = dot(pick, got_ref[...])
        res = (tokens_ref[...].astype(F32) - centres).astype(BF16)
        res_ref[...] = res
        d = iota((D, D), 1)
        place = (
            ((d >> 7) & 1) * 512 + (d >> 8) * 128 + ((d >> 2) & 3) * 32 + ((d >> 4) & 7) * 4
        ) + (d & 3)
        turned_res_ref[...] = dot(one_hot(iota((D, D), 0) == place), res, 1, 1).astype(BF16)

    rotated = dot(res_ref[...], rotation_ref[...])
    left = iota((ROWS, 2 * DSUB), 1) < DSUB
    pieces = []
    for pair in range(2):
        both = rotated[:, pair * 128 : (pair + 1) * 128]
        swapped = pltpu.roll(both, DSUB, 1)
        halves = []
        for side in range(2):
            m = 2 * pair + side
            twice = jnp.where(left, both, swapped) if side == 0 else jnp.where(left, swapped, both)
            high = twice.astype(BF16)
            rest = twice - high.astype(F32)
            low = rest.astype(BF16)
            logits = (2.0 * INV_TEMP) * dot(jnp.concatenate([high, low], axis=1), stack_ref[m]) - norm_ref[m]
            power = jnp.exp(logits - jnp.max(logits, axis=1, keepdims=True))
            prob = power * (1.0 / jnp.sum(power, axis=1, keepdims=True))
            mass = jnp.sum(prob, axis=0, keepdims=True)
            prob = prob.astype(BF16)
            split = jnp.where(left, high.astype(F32), rest).astype(BF16)
            num = dot(split, prob, 0, 0)
            at = pl.ds(pl.multiple_of(step * 256 + m * DSUB, DSUB), DSUB)
            out_ref[at, D : D + K] = (num[:DSUB] + num[DSUB:]).astype(BF16)
            out_ref[at, D + K : D + 2 * K] = jnp.broadcast_to(mass, (DSUB, K)).astype(BF16)
            back = dot(prob, turned_ref[m])
            halves.append(back + pltpu.roll(back, DSUB, 1))
        pieces.append(jnp.where(left, halves[0], halves[1]).astype(BF16))
    cross = dot(turned_res_ref[...], jnp.concatenate(pieces, axis=1)).astype(BF16)
    for q in range(4):
        @pl.when(step == q)
        def _():
            out_ref[:, q * 256 : (q + 1) * 256] = cross


def whole(shape):
    return pl.BlockSpec(shape, lambda *_: (0,) * len(shape))


def find_slots(owner, lists):
    return pl.pallas_call(
        slots_kernel,
        out_shape=(
            jax.ShapeDtypeStruct((ROWS, 1), jnp.int32),
            jax.ShapeDtypeStruct((OWNERS, CAP), jnp.int32),
        ),
        name="slots",
    )(owner, lists.reshape(1, ROWS))


def find_centres(ids, centroids):
    return pl.pallas_call(
        centres_kernel,
        out_shape=jax.ShapeDtypeStruct((OWNERS, CAP, D), BF16),
        name="centres",
    )(ids, centroids)


def split_codes(codebook):
    def block(*shape):
        return pl.BlockSpec((4, *shape), lambda i: (i, 0, 0))

    return pl.pallas_call(
        codes_kernel,
        grid=(M // 4,),
        in_specs=[block(DSUB, K)],
        out_specs=(block(4 * DSUB, K), block(K, 2 * DSUB), block(1, K)),
        out_shape=(
            jax.ShapeDtypeStruct((M, 4 * DSUB, K), BF16),
            jax.ShapeDtypeStruct((M, K, 2 * DSUB), BF16),
            jax.ShapeDtypeStruct((M, 1, K), F32),
        ),
        name="codes",
    )(codebook)


def code_stats(tokens, slot, got, rotation, codes):
    def block(*shape):
        return pl.BlockSpec((4, *shape), lambda i: (i, 0, 0))

    return pl.pallas_call(
        stats_kernel,
        grid=(M // 4,),
        in_specs=[
            whole((ROWS, D)),
            whole((ROWS, 1)),
            whole((OWNERS * CAP, D)),
            pl.BlockSpec((D, 256), lambda i: (0, i)),
            block(4 * DSUB, K),
            block(K, 2 * DSUB),
            block(1, K),
        ],
        out_specs=whole((D, WIDE)),
        out_shape=jax.ShapeDtypeStruct((D, WIDE), BF16),
        scratch_shapes=[pltpu.VMEM((ROWS, D), BF16), pltpu.VMEM((D, ROWS), BF16)],
        name="stats",
    )(tokens, slot, got, rotation, *codes)


def swap(value, axis):
    return lax.all_to_all(value, axis, split_axis=0, concat_axis=0, tiled=True)


def sent_to_all(value, axis):
    copies = jnp.broadcast_to(value, (lax.axis_size(axis), *value.shape))
    return swap(copies, axis).reshape(-1, value.shape[-1])


def local(tokens, owner, list_local, centroids, rotation, codebook):
    slot, ids = find_slots(owner, list_local)
    centres = find_centres(swap(ids, GRP), centroids)
    got = swap(centres, GRP).reshape(OWNERS * CAP, D)
    part = code_stats(tokens, slot, got, rotation, split_codes(codebook))
    part = swap(part.reshape(2, 512, WIDE), "c").astype(F32).sum(axis=0).astype(BF16)
    part = swap(part.reshape(16, 32, WIDE), ("x", "y")).astype(F32).sum(axis=0)
    part = swap(part.reshape(8, 4, WIDE), "z").sum(axis=0)
    cross_cov = part[:, :D] * (1.0 / math.sqrt(ROWS * 256))
    place = (lax.axis_index("c") * 16 + lax.axis_index(("x", "y"))) * 8 + lax.axis_index("z")
    book = lax.dynamic_slice_in_dim(codebook.reshape(M * DSUB, K), place * 4, 4, 0)
    fresh = (part[:, D : D + K] + book) / (part[:, D + K :] + 1.0)
    fresh = sent_to_all(sent_to_all(sent_to_all(fresh, "z"), ("x", "y")), "c")
    return (fresh.reshape(M, DSUB, K), cross_cov)


def solution(mesh):
    finer = Mesh(mesh.devices.reshape(4, 2, 8, 4), ALL)
    in_specs = (P(ALL, None), P(ALL, None), P(ALL), P(ALL, None), P(), P())
    out_specs = (P(), P(ALL, None))
    return jax.shard_map(local, mesh=finer, in_specs=in_specs, out_specs=out_specs, check_vma=False)
```

time: 323 us -> 162 us (0.50); the launches traced: 317 us -> 161 us
  waiting for transfers between devices: 97.9 us -> 39.7 us
  matrix products: 55.7 us -> 0 us
  blocking collectives: 18.9 us -> 63.7 us
  local copies, waits for them, and re-layouts: 46.2 us -> 5.54 us
  starting transfers between devices: 48.5 us -> 16.2 us
  Pallas kernels: 0 us -> 31.9 us
  other arithmetic: 33.5 us -> 3.76 us
  loops' own time: 14.8 us -> 0 us
    all_to_all x7 -> x3, waiting for transfers between devices: 97.9 us -> 39.7 us  [swap(): return lax.all_to_all(value, axis, split_axis=0, concat_axis=0, tiled=True)]
    dot_general x9 -> x0, matrix products: 55.7 us -> none  [the longest x2 16.8 us: one_block(): num = jnp.einsum('smk,smj->mjk', prob, rotated, precision=highest)]
    all_to_all x1 -> x5, blocking collectives: 18.9 us -> 63.7 us  [swap(): return lax.all_to_all(value, axis, split_axis=0, concat_axis=0, tiled=True)]
    all_to_all x7 -> x3, starting transfers between devices: 48.5 us -> 16.2 us  [swap(): return lax.all_to_all(value, axis, split_axis=0, concat_axis=0, tiled=True)]
    pallas_call x0 -> x4, Pallas kernels: none -> 31.9 us  [the longest x1 19.8 us: code_stats(): pl.pallas_call(stats_kernel, grid=(M // 4,), in_specs=[whole((ROWS, D)),...]
    another operation x1 -> x0, loops' own time: 14.8 us -> none  [code_stats(): lax.scan(one_block, start, (residual.reshape(turns, block, feat_width), w...]
    sub x2 -> x0, other arithmetic: 8.98 us -> none  [one_block(): prob = jax.nn.softmax(logits, axis=-1) * row_mask[:, None, None]]
    convert_element_type x5 -> x0, other arithmetic: 8.35 us -> none  [the longest x2 5.47 us: local(): residual = jnp.where(is_valid[:, None], got_rows.astype(jnp.float32) - ce...]
  transfers between devices with their start and end apart: 7 -> 3, of which waited for: 6 -> 3; matrix products, arithmetic and copies ran while one was open for 15% -> 0% of each run, Pallas kernels for 0% -> 2%
where the time goes in v1:
time: 162 us; the launch traced here: 161 us
  blocking collectives  63.7 us (39%)
  waiting for transfers between devices  39.7 us (25%)
  Pallas kernels  31.9 us (20%)
  starting transfers between devices  16.2 us (10%)
  local copies, waits for them, and re-layouts  5.54 us (3%)
  other arithmetic  3.76 us (2%)
    all_to_all x5, blocking collectives, swap(): return lax.all_to_all(value, axis, split_axis=0, concat_axis=0, tiled=True)  63.7 us
    all_to_all x3, waiting for transfers between devices, swap(): return lax.all_to_all(value, axis, split_axis=0, concat_axis=0, tiled=True)  39.7 us
    pallas_call x1, Pallas kernels, code_stats(): pl.pallas_call(stats_kernel, grid=(M // 4,), in_specs=[whole((ROWS, D)),...  19.8 us
    all_to_all x3, starting transfers between devices, swap(): return lax.all_to_all(value, axis, split_axis=0, concat_axis=0, tiled=True)  16.2 us
    pallas_call x1, Pallas kernels, find_centres(): pl.pallas_call(centres_kernel, out_shape=jax.ShapeDtypeStruct((OWNERS, CA...  5.41 us
    unnamed x4, local copies, waits for them, and re-layouts  3.86 us
    pallas_call x1, Pallas kernels, split_codes(): pl.pallas_call(codes_kernel, grid=(M // 4,), in_specs=[block(DSUB, K)], o...  3.79 us
  transfers between devices with their start and end apart: 3, of which 3 were waited for; matrix products, arithmetic and copies ran while one was open for 0% of the time, Pallas kernels for 2%

profile of v1, /device:TPU:1, one launch (start us, length us, event | category | flops | bytes accessed | tf_op | source)
XLA Modules:
  0.0 161.5 jit_solution(7256857741645052269)
XLA Ops:
  0.6 1.5 copy.14.owner_ref
  2.2 2.9 %slots.1 = (s32[512,1]{1,0:T(8,128)}, s32[8,128]{1,0:T(8,128)}) custom-call(s32[512,1]{1,0:T(8,128)} %copy.14.owner_ref, s32[1,512]{1,0:T(1,128)} %bitcast.19), custom_call_target="tpu_custom_call" | custom-call | tf_op jit(solution)/shard_map/slots/pallas_call | solution.py:131
  5.0 11.4 %all_to_all.46 = s32[8,1,128]{2,1,0:T(1,128)} all-to-all(s32[8,1,128]{2,1,0:T(1,128)} %bitcast.18), channel_id=1, replica_groups=mesh['x'=4,'c'=2,'z'=8,'y'=4] {'x','c'}, dimensions={0} | all-to-all | bytes 8192 | tf_op jit(solution)/shard_map/all_to_all | solution.py:191
  16.5 5.4 %centres.1 = bf16[8,128,1024]{2,1,0:T(8,128)(2,1)} custom-call(s32[8,128]{1,0:T(8,128)} %bitcast.17, bf16[1024,1024]{1,0:T(8,128)(2,1)} %centroids_ref.1), custom_call_target="tpu_custom_call" | custom-call | tf_op jit(solution)/shard_map/centres/pallas_call | solution.py:142
  21.9 4.4 %all-to-all-start.1 = ((bf16[8,128,1024]{2,1,0:T(8,128)(2,1)}), bf16[8,128,1024]{2,1,0:T(8,128)(2,1)S(1)}, u32[]{:S(2)}, u32[]{:S(2)}) async-start(bf16[8,128,1024]{2,1,0:T(8,128)(2,1)} %centres.1), calls=%async_computation.1 | async-start | bytes 4194304 | tf_op jit(solution)/shard_map/all_to_all | solution.py:191
  26.2 3.8 %codes.1 = (bf16[16,256,256]{2,1,0:T(8,128)(2,1)}, bf16[16,256,128]{2,1,0:T(8,128)(2,1)}, f32[16,1,256]{2,1,0:T(1,128)}) custom-call(f32[16,64,256]{2,1,0:T(8,128)} %book_ref.1), custom_call_target="tpu_custom_call" | custom-call | tf_op jit(solution)/shard_map/codes/pallas_call | solution.py:153
  30.0 22.6 %all-to-all-done.1 = bf16[8,128,1024]{2,1,0:T(8,128)(2,1)S(1)} async-done(((bf16[8,128,1024]{2,1,0:T(8,128)(2,1)}), bf16[8,128,1024]{2,1,0:T(8,128)(2,1)S(1)}, u32[]{:S(2)}, u32[]{:S(2)}) %all-to-all-start.1) | async-done | bytes 2097184 | tf_op jit(solution)/shard_map/all_to_all | solution.py:191
  52.6 0.0 copy-start
  52.6 1.4 copy-done
  54.0 19.8 %stats.1 = bf16[1024,1536]{1,0:T(8,128)(2,1)} custom-call(bf16[512,1024]{1,0:T(8,128)(2,1)} %tokens_ref.1, s32[512,1]{1,0:T(8,128)} %get-tuple-element.7.slot_ref, bf16[1024,1024]{1,0:T(8,128)(2,1)} %bitcast.12, bf16[1024,1024]{1,0:T(8,128)(2,1)} %rotation_ref.1, bf16[16,256,256]{2,1,0:T(8,128)(2,1)} %get-tuple-element.9.stack_ref, ...), custom_call_target="tpu_custom_call" | custom-call | tf_op jit(solution)/shard_map/stats/pallas_call | solution.py:171
  73.8 8.0 %all_to_all.47 = bf16[2,512,1536]{2,1,0:T(8,128)(2,1)S(1)} all-to-all(bf16[2,512,1536]{2,1,0:T(8,128)(2,1)} %bitcast.11), channel_id=1, replica_groups=mesh['x'=4,'c'=2,'z'=8,'y'=4] {'c'}, dimensions={0} | all-to-all | bytes 6291456 | tf_op jit(solution)/shard_map/all_to_all | solution.py:191
  81.8 2.2 %reduce_sum.30 = bf16[512,1536]{1,0:T(8,128)(2,1)} reduce(bf16[2,512,1536]{2,1,0:T(8,128)(2,1)S(1)} %all_to_all.47, bf16[]{:T(256)} %constant.8.clone.1), dimensions={0}, to_apply=%region_0.0 | reduce | flops 786432 | bytes 4718594 | tf_op jit(solution)/shard_map/reduce_sum | solution.py:204
  84.0 25.3 %all_to_all.48 = bf16[16,32,1536]{2,1,0:T(8,128)(2,1)S(1)} all-to-all(bf16[16,32,1536]{2,1,0:T(8,128)(2,1)} %bitcast.13), channel_id=1, replica_groups=mesh['x'=4,'c'=2,'z'=8,'y'=4] {'x','y'}, dimensions={0} | all-to-all | bytes 3145728 | tf_op jit(solution)/shard_map/all_to_all | solution.py:191
  109.3 0.2 convert_reduce_fusion
  109.5 0.7 reshape.34
  110.2 8.2 %all-to-all-start.4 = ((f32[8,4,1536]{2,1,0:T(4,128)}), f32[8,4,1536]{2,1,0:T(4,128)S(1)}, u32[]{:S(2)}, u32[]{:S(2)}) async-start(f32[8,4,1536]{2,1,0:T(4,128)} %reshape.34), calls=%async_computation.4 | async-start | bytes 393216 | tf_op jit(solution)/shard_map/all_to_all | solution.py:191
  118.4 8.7 %all-to-all-done.4 = f32[8,4,1536]{2,1,0:T(4,128)S(1)} async-done(((f32[8,4,1536]{2,1,0:T(4,128)}), f32[8,4,1536]{2,1,0:T(4,128)S(1)}, u32[]{:S(2)}, u32[]{:S(2)}) %all-to-all-start.4) | async-done | bytes 196640 | tf_op jit(solution)/shard_map/all_to_all | solution.py:191
  127.2 0.7 fusion
  127.9 9.2 %all_to_all.49 = f32[8,4,256]{2,1,0:T(4,128)S(1)} all-to-all(f32[8,4,256]{2,1,0:T(4,128)S(1)} %broadcast_in_dim.9), channel_id=1, replica_groups=mesh['x'=4,'c'=2,'z'=8,'y'=4] {'z'}, dimensions={0} | all-to-all | bytes 65536 | tf_op jit(solution)/shard_map/all_to_all | solution.py:191
  137.2 0.8 broadcast_in_dim.10
  138.0 3.7 %all-to-all-start.6 = ((f32[16,32,256]{2,1,0:T(8,128)}), f32[16,32,256]{2,1,0:T(8,128)S(1)}, u32[]{:S(2)}, u32[]{:S(2)}) async-start(f32[16,32,256]{2,1,0:T(8,128)} %broadcast_in_dim.10), calls=%async_computation.6 | async-start | bytes 1048576 | tf_op jit(solution)/shard_map/all_to_all | solution.py:191
  141.7 0.6 slice_multiply_fusion
  142.4 8.3 %all-to-all-done.6 = f32[16,32,256]{2,1,0:T(8,128)S(1)} async-done(((f32[16,32,256]{2,1,0:T(8,128)}), f32[16,32,256]{2,1,0:T(8,128)S(1)}, u32[]{:S(2)}, u32[]{:S(2)}) %all-to-all-start.6) | async-done | bytes 524320 | tf_op jit(solution)/shard_map/all_to_all | solution.py:191
  150.7 0.1 broadcast_in_dim.11
  150.8 9.7 %all_to_all.50 = f32[2,512,256]{2,1,0:T(8,128)S(1)} all-to-all(f32[2,512,256]{2,1,0:T(8,128)S(1)} %broadcast_in_dim.11), channel_id=1, replica_groups=mesh['x'=4,'c'=2,'z'=8,'y'=4] {'c'}, dimensions={0} | all-to-all | bytes 2097152 | tf_op jit(solution)/shard_map/all_to_all | solution.py:191
  160.5 1.0 copy.22
  (3 shorter events, 0.1 us)
Async XLA Ops:
  21.9 30.7 %all-to-all-start.1 = ((bf16[8,128,1024]{2,1,0:T(8,128)(2,1)}), bf16[8,128,1024]{2,1,0:T(8,128)(2,1)S(1)}, u32[]{:S(2)}, u32[]{:S(2)}) async-start(bf16[8,128,1024]{2,1,0:T(8,128)(2,1)} %centres.1), calls=%async_computation.1 | async-start | bytes 4194304 | tf_op jit(solution)/shard_map/all_to_all | solution.py:191
  52.6 1.4 copy-start
  110.2 16.9 %all-to-all-start.4 = ((f32[8,4,1536]{2,1,0:T(4,128)}), f32[8,4,1536]{2,1,0:T(4,128)S(1)}, u32[]{:S(2)}, u32[]{:S(2)}) async-start(f32[8,4,1536]{2,1,0:T(4,128)} %reshape.34), calls=%async_computation.4 | async-start | bytes 393216 | tf_op jit(solution)/shard_map/all_to_all | solution.py:191
  138.0 12.7 %all-to-all-start.6 = ((f32[16,32,256]{2,1,0:T(8,128)}), f32[16,32,256]{2,1,0:T(8,128)S(1)}, u32[]{:S(2)}, u32[]{:S(2)}) async-start(f32[16,32,256]{2,1,0:T(8,128)} %broadcast_in_dim.10), calls=%async_computation.6 | async-start | bytes 1048576 | tf_op jit(solution)/shard_map/all_to_all | solution.py:191

commit v2 on v1

--- a/solution.py
+++ b/solution.py
@@ -10,6 +10,7 @@
 
 ALL = ("x", "c", "z", "y")
 GRP = ("x", "c")
+XY = ("x", "y")
 OWNERS = 8
 CAP = 128
 LISTS = 1024
@@ -18,7 +19,7 @@
 M = 16
 DSUB = 64
 K = 256
-WIDE = D + 2 * K
+WIDE = D + K + 128
 INV_TEMP = 0.2
 F32 = jnp.float32
 BF16 = jnp.bfloat16
@@ -112,7 +113,9 @@
             num = dot(split, prob, 0, 0)
             at = pl.ds(pl.multiple_of(step * 256 + m * DSUB, DSUB), DSUB)
             out_ref[at, D : D + K] = (num[:DSUB] + num[DSUB:]).astype(BF16)
-            out_ref[at, D + K : D + 2 * K] = jnp.broadcast_to(mass, (DSUB, K)).astype(BF16)
+            row = iota((DSUB, 128), 0) % 32
+            masses = jnp.where(row == 0, mass[:, :128], jnp.where(row == 1, mass[:, 128:], 0.0))
+            out_ref[at, D + K :] = masses.astype(BF16)
             back = dot(prob, turned_ref[m])
             halves.append(back + pltpu.roll(back, DSUB, 1))
         pieces.append(jnp.where(left, halves[0], halves[1]).astype(BF16))
@@ -121,6 +124,43 @@
         @pl.when(step == q)
         def _():
             out_ref[:, q * 256 : (q + 1) * 256] = cross
+
+
+def pack_kernel(part_ref, out_ref):
+    total = part_ref[0].astype(F32)
+    for i in range(1, 16):
+        total = total + part_ref[i].astype(F32)
+    mass = jnp.concatenate([total[0:1, D + K :], total[1:2, D + K :], jnp.zeros((1, D - K), F32)], axis=1)
+    mass = jnp.broadcast_to(mass, (4, D))
+    num = jnp.concatenate([total[8 * b : 8 * b + 8, D : D + K] for b in range(4)], axis=1)
+    for z in range(8):
+        head = jnp.concatenate([total[4 * z : 4 * z + 4, :D], mass], axis=0)
+        out_ref[z] = jnp.concatenate([head, num], axis=0).astype(BF16)
+
+
+def finish_kernel(part_ref, book_ref, cross_ref, fresh_ref):
+    total = part_ref[0].astype(F32)
+    for i in range(1, 8):
+        total = total + part_ref[i].astype(F32)
+    cross_ref[...] = total[0:4] * (1.0 / math.sqrt(ROWS * 256))
+    count = total[4:5, :K] + 1.0
+    for b in range(4):
+        at = slice(8 * b, 8 * b + 8)
+        fresh_ref[at] = (total[8:16, b * K : (b + 1) * K] + book_ref[at]) / count
+
+
+def pack(part):
+    return pl.pallas_call(
+        pack_kernel, out_shape=jax.ShapeDtypeStruct((8, 16, D), BF16), name="pack"
+    )(part)
+
+
+def finish(part, book):
+    return pl.pallas_call(
+        finish_kernel,
+        out_shape=(jax.ShapeDtypeStruct((4, D), F32), jax.ShapeDtypeStruct((32, K), F32)),
+        name="finish",
+    )(part, book)
 
 
 def whole(shape):
@@ -202,13 +242,11 @@
     got = swap(centres, GRP).reshape(OWNERS * CAP, D)
     part = code_stats(tokens, slot, got, rotation, split_codes(codebook))
     part = swap(part.reshape(2, 512, WIDE), "c").astype(F32).sum(axis=0).astype(BF16)
-    part = swap(part.reshape(16, 32, WIDE), ("x", "y")).astype(F32).sum(axis=0)
-    part = swap(part.reshape(8, 4, WIDE), "z").sum(axis=0)
-    cross_cov = part[:, :D] * (1.0 / math.sqrt(ROWS * 256))
-    place = (lax.axis_index("c") * 16 + lax.axis_index(("x", "y"))) * 8 + lax.axis_index("z")
-    book = lax.dynamic_slice_in_dim(codebook.reshape(M * DSUB, K), place * 4, 4, 0)
-    fresh = (part[:, D : D + K] + book) / (part[:, D + K :] + 1.0)
-    fresh = sent_to_all(sent_to_all(sent_to_all(fresh, "z"), ("x", "y")), "c")
+    part = swap(pack(swap(part.reshape(16, 32, WIDE), XY)), "z")
+    place = lax.axis_index("c") * 16 + lax.axis_index(XY)
+    book = lax.dynamic_slice_in_dim(codebook.reshape(M * DSUB, K), place * 32, 32, 0)
+    cross_cov, fresh = finish(part, book)
+    fresh = sent_to_all(sent_to_all(fresh, XY), "c")
     return (fresh.reshape(M, DSUB, K), cross_cov)
 
 

time: 162 us -> 154 us (0.951)
  waiting for transfers between devices: 39.7 us -> 30.6 us
  starting transfers between devices: 16.2 us -> 11.3 us
  Pallas kernels: 31.9 us -> 35.7 us
  blocking collectives: 63.7 us -> 66 us
  other arithmetic: 3.76 us -> 2.05 us
    all_to_all x3 -> x2, waiting for transfers between devices: 39.7 us -> 30.6 us  [swap(): return lax.all_to_all(value, axis, split_axis=0, concat_axis=0, tiled=True)]
    all_to_all x3 -> x2, starting transfers between devices: 16.2 us -> 11.3 us  [swap(): return lax.all_to_all(value, axis, split_axis=0, concat_axis=0, tiled=True)]
    pallas_call x0 -> x2, Pallas kernels: none -> 3.85 us  [the longest x1 2.26 us: pack(): pl.pallas_call(pack_kernel, out_shape=jax.ShapeDtypeStruct((8, 16, D), BF...]
    all_to_all x5, blocking collectives: 63.7 us -> 66 us  [swap(): return lax.all_to_all(value, axis, split_axis=0, concat_axis=0, tiled=True)]
    unnamed x4 -> x6, local copies, waits for them, and re-layouts: 3.86 us -> 4.56 us
  transfers between devices with their start and end apart: 3 -> 2, of which waited for: 3 -> 2; matrix products, arithmetic and copies ran while one was open for 0% -> 1% of each run, Pallas kernels for 2% -> 2%
where the time goes in v2:
time: 154 us; the launch traced here: 153 us
  blocking collectives  66 us (43%)
  Pallas kernels  35.7 us (23%)
  waiting for transfers between devices  30.6 us (20%)
  starting transfers between devices  11.3 us (7%)
  local copies, waits for them, and re-layouts  6.8 us (4%)
  other arithmetic  2.05 us (1%)
    all_to_all x5, blocking collectives, swap(): return lax.all_to_all(value, axis, split_axis=0, concat_axis=0, tiled=True)  66 us
    all_to_all x2, waiting for transfers between devices, swap(): return lax.all_to_all(value, axis, split_axis=0, concat_axis=0, tiled=True)  30.6 us
    pallas_call x1, Pallas kernels, code_stats(): pl.pallas_call(stats_kernel, grid=(M // 4,), in_specs=[whole((ROWS, D)),...  19.7 us
    all_to_all x2, starting transfers between devices, swap(): return lax.all_to_all(value, axis, split_axis=0, concat_axis=0, tiled=True)  11.3 us
    pallas_call x1, Pallas kernels, find_centres(): pl.pallas_call(centres_kernel, out_shape=jax.ShapeDtypeStruct((OWNERS, CA...  5.42 us
    unnamed x6, local copies, waits for them, and re-layouts  4.56 us
    pallas_call x1, Pallas kernels, split_codes(): pl.pallas_call(codes_kernel, grid=(M // 4,), in_specs=[block(DSUB, K)], o...  3.79 us
  transfers between devices with their start and end apart: 2, of which 2 were waited for; matrix products, arithmetic and copies ran while one was open for 1% of the time, Pallas kernels for 2%

profile of v2, /device:TPU:1, one launch (start us, length us, event | category | flops | bytes accessed | tf_op | source)
XLA Modules:
  0.0 153.1 jit_solution(4845922995412474444)
XLA Ops:
  0.6 1.5 %copy.9.owner_ref = s32[512,1]{1,0:T(8,128)} copy(s32[512,1]{0,1:T(1,128)} %param.7) | data formatting | bytes 4096 | tf_op args[1]
  2.2 2.9 %slots.1 = (s32[512,1]{1,0:T(8,128)}, s32[8,128]{1,0:T(8,128)}) custom-call(s32[512,1]{1,0:T(8,128)} %copy.9.owner_ref, s32[1,512]{1,0:T(1,128)} %bitcast.19), custom_call_target="tpu_custom_call" | custom-call | tf_op jit(solution)/shard_map/slots/pallas_call | solution.py:171
  5.0 11.5 %all_to_all.41 = s32[8,1,128]{2,1,0:T(1,128)} all-to-all(s32[8,1,128]{2,1,0:T(1,128)} %bitcast.18), channel_id=1, replica_groups=mesh['x'=4,'c'=2,'z'=8,'y'=4] {'x','c'}, dimensions={0} | all-to-all | bytes 8192 | tf_op jit(solution)/shard_map/all_to_all | solution.py:231
  16.5 5.4 %centres.1 = bf16[8,128,1024]{2,1,0:T(8,128)(2,1)} custom-call(s32[8,128]{1,0:T(8,128)} %bitcast.17, bf16[1024,1024]{1,0:T(8,128)(2,1)} %centroids_ref.1), custom_call_target="tpu_custom_call" | custom-call | tf_op jit(solution)/shard_map/centres/pallas_call | solution.py:182
  21.9 4.4 %all-to-all-start.1 = ((bf16[8,128,1024]{2,1,0:T(8,128)(2,1)}), bf16[8,128,1024]{2,1,0:T(8,128)(2,1)S(1)}, u32[]{:S(2)}, u32[]{:S(2)}) async-start(bf16[8,128,1024]{2,1,0:T(8,128)(2,1)} %centres.1), calls=%async_computation.1 | async-start | bytes 4194304 | tf_op jit(solution)/shard_map/all_to_all | solution.py:231
  26.3 3.8 %codes.1 = (bf16[16,256,256]{2,1,0:T(8,128)(2,1)}, bf16[16,256,128]{2,1,0:T(8,128)(2,1)}, f32[16,1,256]{2,1,0:T(1,128)}) custom-call(f32[16,64,256]{2,1,0:T(8,128)} %book_ref.1), custom_call_target="tpu_custom_call" | custom-call | tf_op jit(solution)/shard_map/codes/pallas_call | solution.py:193
  30.1 22.6 %all-to-all-done.1 = bf16[8,128,1024]{2,1,0:T(8,128)(2,1)S(1)} async-done(((bf16[8,128,1024]{2,1,0:T(8,128)(2,1)}), bf16[8,128,1024]{2,1,0:T(8,128)(2,1)S(1)}, u32[]{:S(2)}, u32[]{:S(2)}) %all-to-all-start.1) | async-done | bytes 2097184 | tf_op jit(solution)/shard_map/all_to_all | solution.py:231
  52.6 0.0 copy-start
  52.6 1.4 copy-done
  54.0 19.7 %stats.1 = bf16[1024,1408]{1,0:T(8,128)(2,1)} custom-call(bf16[512,1024]{1,0:T(8,128)(2,1)} %tokens_ref.1, s32[512,1]{1,0:T(8,128)} %get-tuple-element.9.slot_ref, bf16[1024,1024]{1,0:T(8,128)(2,1)} %bitcast.12, bf16[1024,1024]{1,0:T(8,128)(2,1)} %rotation_ref.1, bf16[16,256,256]{2,1,0:T(8,128)(2,1)} %get-tuple-element.11.stack_ref, ...), custom_call_target="tpu_custom_call" | custom-call | tf_op jit(solution)/shard_map/stats/pallas_call | solution.py:211
  73.7 7.8 %all_to_all.42 = bf16[2,512,1408]{2,1,0:T(8,128)(2,1)S(1)} all-to-all(bf16[2,512,1408]{2,1,0:T(8,128)(2,1)} %bitcast.11), channel_id=1, replica_groups=mesh['x'=4,'c'=2,'z'=8,'y'=4] {'c'}, dimensions={0} | all-to-all | bytes 5767168 | tf_op jit(solution)/shard_map/all_to_all | solution.py:231
  81.5 2.0 %reduce_sum.12 = bf16[512,1408]{1,0:T(8,128)(2,1)} reduce(bf16[2,512,1408]{2,1,0:T(8,128)(2,1)S(1)} %all_to_all.42, bf16[]{:T(256)} %constant.10.clone.1), dimensions={0}, to_apply=%region_0.0 | reduce | flops 720896 | bytes 4325378 | tf_op jit(solution)/shard_map/reduce_sum | solution.py:244
  83.6 24.7 %all_to_all.43.part_ref = bf16[16,32,1408]{2,1,0:T(8,128)(2,1)} all-to-all(bf16[16,32,1408]{2,1,0:T(8,128)(2,1)} %bitcast.13), channel_id=1, replica_groups=mesh['x'=4,'c'=2,'z'=8,'y'=4] {'x','y'}, dimensions={0} | all-to-all | bytes 2883584 | tf_op jit(solution)/shard_map/all_to_all | solution.py:231
  108.3 2.3 %pack.1 = bf16[8,16,1024]{2,1,0:T(8,128)(2,1)} custom-call(bf16[16,32,1408]{2,1,0:T(8,128)(2,1)} %all_to_all.43.part_ref), custom_call_target="tpu_custom_call" | custom-call | tf_op jit(solution)/shard_map/pack/pallas_call | solution.py:153
  110.5 6.9 %all-to-all-start.4 = ((bf16[8,16,1024]{2,1,0:T(8,128)(2,1)}), bf16[8,16,1024]{2,1,0:T(8,128)(2,1)S(1)}, u32[]{:S(2)}, u32[]{:S(2)}) async-start(bf16[8,16,1024]{2,1,0:T(8,128)(2,1)} %pack.1), calls=%async_computation.4 | async-start | bytes 524288 | tf_op jit(solution)/shard_map/all_to_all | solution.py:231
  117.5 1.4 constant_dynamic-slice_fusion.book_ref
  118.8 8.0 %all-to-all-done.4.part_ref = bf16[8,16,1024]{2,1,0:T(8,128)(2,1)S(1)} async-done(((bf16[8,16,1024]{2,1,0:T(8,128)(2,1)}), bf16[8,16,1024]{2,1,0:T(8,128)(2,1)S(1)}, u32[]{:S(2)}, u32[]{:S(2)}) %all-to-all-start.4) | async-done | bytes 262176 | tf_op jit(solution)/shard_map/all_to_all | solution.py:231
  126.9 0.0 copy-start.1
  126.9 0.7 copy-done.1
  127.6 1.6 %finish.1 = (f32[4,1024]{1,0:T(4,128)}, f32[32,256]{1,0:T(8,128)}) custom-call(bf16[8,16,1024]{2,1,0:T(8,128)(2,1)} %copy-done.1, f32[32,256]{1,0:T(8,128)} %constant_dynamic-slice_fusion.book_ref), custom_call_target="tpu_custom_call" | custom-call | tf_op jit(solution)/shard_map/finish/pallas_call | solution.py:159
  129.2 0.8 broadcast_in_dim.6
  130.0 13.0 %all_to_all.44 = f32[16,32,256]{2,1,0:T(8,128)S(1)} all-to-all(f32[16,32,256]{2,1,0:T(8,128)S(1)} %broadcast_in_dim.6), channel_id=1, replica_groups=mesh['x'=4,'c'=2,'z'=8,'y'=4] {'x','y'}, dimensions={0} | all-to-all | bytes 1048576 | tf_op jit(solution)/shard_map/all_to_all | solution.py:231
  143.0 0.1 broadcast_in_dim.7
  143.1 9.0 %all_to_all.45 = f32[2,512,256]{2,1,0:T(8,128)S(1)} all-to-all(f32[2,512,256]{2,1,0:T(8,128)S(1)} %broadcast_in_dim.7), channel_id=1, replica_groups=mesh['x'=4,'c'=2,'z'=8,'y'=4] {'c'}, dimensions={0} | all-to-all | bytes 2097152 | tf_op jit(solution)/shard_map/all_to_all | solution.py:231
  152.1 1.0 copy.12
Async XLA Ops:
  21.9 30.7 %all-to-all-start.1 = ((bf16[8,128,1024]{2,1,0:T(8,128)(2,1)}), bf16[8,128,1024]{2,1,0:T(8,128)(2,1)S(1)}, u32[]{:S(2)}, u32[]{:S(2)}) async-start(bf16[8,128,1024]{2,1,0:T(8,128)(2,1)} %centres.1), calls=%async_computation.1 | async-start | bytes 4194304 | tf_op jit(solution)/shard_map/all_to_all | solution.py:231
  52.6 1.4 copy-start
  110.5 16.3 %all-to-all-start.4 = ((bf16[8,16,1024]{2,1,0:T(8,128)(2,1)}), bf16[8,16,1024]{2,1,0:T(8,128)(2,1)S(1)}, u32[]{:S(2)}, u32[]{:S(2)}) async-start(bf16[8,16,1024]{2,1,0:T(8,128)(2,1)} %pack.1), calls=%async_computation.4 | async-start | bytes 524288 | tf_op jit(solution)/shard_map/all_to_all | solution.py:231
  126.9 0.7 copy-start.1

commit v3 on v2

--- a/solution.py
+++ b/solution.py
@@ -1,4 +1,5 @@
 import math
+from functools import partial
 
 import jax
 import jax.numpy as jnp
@@ -15,6 +16,8 @@
 CAP = 128
 LISTS = 1024
 ROWS = 512
+HALF = 256
+SLOTS = 512
 D = 1024
 M = 16
 DSUB = 64
@@ -37,29 +40,38 @@
     return jnp.where(hit, 1.0, 0.0).astype(BF16)
 
 
-def slots_kernel(owner_ref, lists_ref, slot_ref, ids_ref):
+def as_row(column):
+    return jnp.broadcast_to(column, (ROWS, 128)).T[0:1]
+
+
+def slots_kernel(owner_ref, lists_ref, slot_ref, rank_ref, ids_ref):
     owner = owner_ref[...]
     mine = owner == iota((ROWS, 128), 1)
     earlier = one_hot(iota((ROWS, ROWS), 0) > iota((ROWS, ROWS), 1))
     before = dot(earlier, one_hot(mine))
     position = jnp.sum(jnp.where(mine, before, 0.0), axis=1, keepdims=True)
-    slot = owner * CAP + position.astype(jnp.int32)
-    slot_ref[...] = slot
     lists = lists_ref[...]
     row = iota((8, ROWS), 0)
     parts = jnp.where(row == 0, lists >> 5, jnp.where(row == 1, lists & 31, 1))
-    sent = dot(parts.astype(F32).astype(BF16), one_hot(slot == iota((ROWS, OWNERS * CAP), 1)))
+    target = owner * CAP + position.astype(jnp.int32)
+    sent = dot(parts.astype(F32).astype(BF16), one_hot(target == iota((ROWS, OWNERS * CAP), 1)))
     ids = sent[0:1] * 32.0 + sent[1:2] + sent[2:3] - 1.0
     for o in range(OWNERS):
         ids_ref[o : o + 1, :] = ids[:, o * CAP : (o + 1) * CAP].astype(jnp.int32)
-
-
-def centres_kernel(ids_ref, centroids_ref, out_ref):
+    key = position * ROWS + iota((ROWS, 1), 0).astype(F32)
+    lower = jnp.where(jnp.broadcast_to(key, (ROWS, ROWS)) < as_row(key), 1.0, 0.0)
+    rank_ref[...] = jnp.sum(lower, axis=0, keepdims=True).astype(jnp.int32)
+    late = jnp.where(position >= 64.0, SLOTS - 64.0, 0.0)
+    slot = owner.astype(F32) * 64.0 + position + late
+    slot_ref[...] = as_row(slot).astype(jnp.int32)
+
+
+def centres_kernel(half, ids_ref, centroids_ref, out_ref):
     ids = ids_ref[...].astype(F32).T.astype(jnp.int32)
     table = centroids_ref[...]
     for s in range(OWNERS):
-        pick = one_hot(ids[:, s : s + 1] == iota((CAP, LISTS), 1))
-        out_ref[s] = dot(pick, table).astype(BF16)
+        mine = ids[half * 64 : half * 64 + 64, s : s + 1]
+        out_ref[s] = dot(one_hot(mine == iota((64, LISTS), 1)), table).astype(BF16)
 
 
 def codes_kernel(book_ref, stack_ref, turned_ref, norm_ref):
@@ -73,26 +85,27 @@
         norm_ref[i] = INV_TEMP * jnp.sum(book * book, axis=0, keepdims=True)
 
 
-def stats_kernel(
-    tokens_ref, slot_ref, got_ref, rotation_ref, stack_ref, turned_ref, norm_ref,
-    out_ref, res_ref, turned_res_ref,
-):
-    step = pl.program_id(0)
-
-    @pl.when(step == 0)
-    def _():
-        pick = one_hot(slot_ref[...] == iota((ROWS, OWNERS * CAP), 1))
-        centres = dot(pick, got_ref[...])
-        res = (tokens_ref[...].astype(F32) - centres).astype(BF16)
-        res_ref[...] = res
-        d = iota((D, D), 1)
-        place = (
-            ((d >> 7) & 1) * 512 + (d >> 8) * 128 + ((d >> 2) & 3) * 32 + ((d >> 4) & 7) * 4
-        ) + (d & 3)
-        turned_res_ref[...] = dot(one_hot(iota((D, D), 0) == place), res, 1, 1).astype(BF16)
-
+def residuals(half, tokens_ref, rank_ref, slot_ref, gots):
+    chosen = rank_ref[...] == iota((HALF, ROWS), 0) + half * HALF
+    rows = dot(one_hot(chosen), tokens_ref[...])
+    slot = jnp.sum(jnp.where(chosen, slot_ref[...], 0), axis=1, keepdims=True)
+    centres = jnp.zeros((HALF, D), F32)
+    for i, got_ref in enumerate(gots):
+        centres += dot(one_hot(slot == iota((HALF, SLOTS), 1) + i * SLOTS), got_ref[...])
+    return (rows - centres).astype(BF16)
+
+
+def turned_and_placed(res):
+    d = iota((D, D), 1)
+    place = (
+        ((d >> 7) & 1) * 512 + (d >> 8) * 128 + ((d >> 2) & 3) * 32 + ((d >> 4) & 7) * 4
+    ) + (d & 3)
+    return dot(one_hot(iota((D, D), 0) == place), res, 1, 1).astype(BF16)
+
+
+def four_codes(res_ref, rotation_ref, stack_ref, turned_ref, norm_ref, write):
     rotated = dot(res_ref[...], rotation_ref[...])
-    left = iota((ROWS, 2 * DSUB), 1) < DSUB
+    left = iota((HALF, 2 * DSUB), 1) < DSUB
     pieces = []
     for pair in range(2):
         both = rotated[:, pair * 128 : (pair + 1) * 128]
@@ -111,15 +124,52 @@
             prob = prob.astype(BF16)
             split = jnp.where(left, high.astype(F32), rest).astype(BF16)
             num = dot(split, prob, 0, 0)
-            at = pl.ds(pl.multiple_of(step * 256 + m * DSUB, DSUB), DSUB)
-            out_ref[at, D : D + K] = (num[:DSUB] + num[DSUB:]).astype(BF16)
             row = iota((DSUB, 128), 0) % 32
             masses = jnp.where(row == 0, mass[:, :128], jnp.where(row == 1, mass[:, 128:], 0.0))
-            out_ref[at, D + K :] = masses.astype(BF16)
+            at = pl.ds(pl.multiple_of(pl.program_id(0) * 256 + m * DSUB, DSUB), DSUB)
+            write(at, num[:DSUB] + num[DSUB:], masses)
             back = dot(prob, turned_ref[m])
             halves.append(back + pltpu.roll(back, DSUB, 1))
         pieces.append(jnp.where(left, halves[0], halves[1]).astype(BF16))
-    cross = dot(turned_res_ref[...], jnp.concatenate(pieces, axis=1)).astype(BF16)
+    return jnp.concatenate(pieces, axis=1)
+
+
+def first_stats_kernel(
+    tokens_ref, rank_ref, slot_ref, early_ref, rotation_ref, stack_ref, turned_ref, norm_ref,
+    num_ref, back_ref, placed_ref, res_ref,
+):
+    @pl.when(pl.program_id(0) == 0)
+    def _():
+        res = residuals(0, tokens_ref, rank_ref, slot_ref, (early_ref,))
+        res_ref[...] = res
+        placed_ref[...] = turned_and_placed(res)
+
+    def write(at, num, masses):
+        num_ref[at, :K] = num
+        num_ref[at, K:] = masses
+
+    back_ref[...] = four_codes(res_ref, rotation_ref, stack_ref, turned_ref, norm_ref, write)
+
+
+def second_stats_kernel(
+    tokens_ref, rank_ref, slot_ref, early_ref, late_ref, rotation_ref, stack_ref, turned_ref, norm_ref,
+    num_ref, back_ref, placed_ref, out_ref, res_ref, placed_too_ref,
+):
+    step = pl.program_id(0)
+
+    @pl.when(step == 0)
+    def _():
+        res = residuals(1, tokens_ref, rank_ref, slot_ref, (early_ref, late_ref))
+        res_ref[...] = res
+        placed_too_ref[...] = turned_and_placed(res)
+
+    def write(at, num, masses):
+        out_ref[at, D : D + K] = (num + num_ref[at, :K]).astype(BF16)
+        out_ref[at, D + K :] = (masses + num_ref[at, K:]).astype(BF16)
+
+    back = four_codes(res_ref, rotation_ref, stack_ref, turned_ref, norm_ref, write)
+    cross = dot(placed_ref[...], back_ref[...]) + dot(placed_too_ref[...], back)
+    cross = cross.astype(BF16)
     for q in range(4):
         @pl.when(step == q)
         def _():
@@ -135,13 +185,13 @@
     num = jnp.concatenate([total[8 * b : 8 * b + 8, D : D + K] for b in range(4)], axis=1)
     for z in range(8):
         head = jnp.concatenate([total[4 * z : 4 * z + 4, :D], mass], axis=0)
-        out_ref[z] = jnp.concatenate([head, num], axis=0).astype(BF16)
+        out_ref[z] = jnp.concatenate([head, num], axis=0)
 
 
 def finish_kernel(part_ref, book_ref, cross_ref, fresh_ref):
-    total = part_ref[0].astype(F32)
+    total = part_ref[0]
     for i in range(1, 8):
-        total = total + part_ref[i].astype(F32)
+        total = total + part_ref[i]
     cross_ref[...] = total[0:4] * (1.0 / math.sqrt(ROWS * 256))
     count = total[4:5, :K] + 1.0
     for b in range(4):
@@ -151,7 +201,7 @@
 
 def pack(part):
     return pl.pallas_call(
-        pack_kernel, out_shape=jax.ShapeDtypeStruct((8, 16, D), BF16), name="pack"
+        pack_kernel, out_shape=jax.ShapeDtypeStruct((8, 16, D), F32), name="pack"
     )(part)
 
 
@@ -168,20 +218,18 @@
 
 
 def find_slots(owner, lists):
+    line = jax.ShapeDtypeStruct((1, ROWS), jnp.int32)
     return pl.pallas_call(
         slots_kernel,
-        out_shape=(
-            jax.ShapeDtypeStruct((ROWS, 1), jnp.int32),
-            jax.ShapeDtypeStruct((OWNERS, CAP), jnp.int32),
-        ),
+        out_shape=(line, line, jax.ShapeDtypeStruct((OWNERS, CAP), jnp.int32)),
         name="slots",
     )(owner, lists.reshape(1, ROWS))
 
 
-def find_centres(ids, centroids):
-    return pl.pallas_call(
-        centres_kernel,
-        out_shape=jax.ShapeDtypeStruct((OWNERS, CAP, D), BF16),
+def find_centres(half, ids, centroids):
+    return pl.pallas_call(
+        partial(centres_kernel, half),
+        out_shape=jax.ShapeDtypeStruct((OWNERS, 64, D), BF16),
         name="centres",
     )(ids, centroids)
 
@@ -204,27 +252,38 @@
     )(codebook)
 
 
-def code_stats(tokens, slot, got, rotation, codes):
+def code_stats(rows, gots, rotation, codes, before=()):
     def block(*shape):
         return pl.BlockSpec((4, *shape), lambda i: (i, 0, 0))
 
-    return pl.pallas_call(
-        stats_kernel,
+    columns = pl.BlockSpec((HALF, 256), lambda i: (0, i))
+    sums = [whole((D, K + 128)), columns, whole((D, HALF))]
+    placed = pltpu.VMEM((D, HALF), BF16)
+    first = not before
+    shapes = (
+        jax.ShapeDtypeStruct((D, K + 128), F32),
+        jax.ShapeDtypeStruct((HALF, D), BF16),
+        jax.ShapeDtypeStruct((D, HALF), BF16),
+    )
+    return pl.pallas_call(
+        first_stats_kernel if first else second_stats_kernel,
         grid=(M // 4,),
         in_specs=[
             whole((ROWS, D)),
-            whole((ROWS, 1)),
-            whole((OWNERS * CAP, D)),
+            whole((1, ROWS)),
+            whole((1, ROWS)),
+            *[whole((SLOTS, D)) for _ in gots],
             pl.BlockSpec((D, 256), lambda i: (0, i)),
             block(4 * DSUB, K),
             block(K, 2 * DSUB),
             block(1, K),
+            *([] if first else sums),
         ],
-        out_specs=whole((D, WIDE)),
-        out_shape=jax.ShapeDtypeStruct((D, WIDE), BF16),
-        scratch_shapes=[pltpu.VMEM((ROWS, D), BF16), pltpu.VMEM((D, ROWS), BF16)],
-        name="stats",
-    )(tokens, slot, got, rotation, *codes)
+        out_specs=tuple(sums) if first else whole((D, WIDE)),
+        out_shape=shapes if first else jax.ShapeDtypeStruct((D, WIDE), BF16),
+        scratch_shapes=[pltpu.VMEM((HALF, D), BF16)] + ([] if first else [placed]),
+        name="first_stats" if first else "second_stats",
+    )(*rows, *gots, rotation, *codes, *before)
 
 
 def swap(value, axis):
@@ -237,10 +296,14 @@
 
 
 def local(tokens, owner, list_local, centroids, rotation, codebook):
-    slot, ids = find_slots(owner, list_local)
-    centres = find_centres(swap(ids, GRP), centroids)
-    got = swap(centres, GRP).reshape(OWNERS * CAP, D)
-    part = code_stats(tokens, slot, got, rotation, split_codes(codebook))
+    slot, rank, ids = find_slots(owner, list_local)
+    ids = swap(ids, GRP)
+    early = swap(find_centres(0, ids, centroids), GRP).reshape(SLOTS, D)
+    late = swap(find_centres(1, ids, centroids), GRP).reshape(SLOTS, D)
+    rows = (tokens, rank, slot)
+    codes = split_codes(codebook)
+    before = code_stats(rows, (early,), rotation, codes)
+    part = code_stats(rows, (early, late), rotation, codes, before)
     part = swap(part.reshape(2, 512, WIDE), "c").astype(F32).sum(axis=0).astype(BF16)
     part = swap(pack(swap(part.reshape(16, 32, WIDE), XY)), "z")
     place = lax.axis_index("c") * 16 + lax.axis_index(XY)

time: 154 us -> 170 us (1.10)
  Pallas kernels: 35.7 us -> 53.8 us
  waiting for transfers between devices: 30.6 us -> 22.8 us
  starting transfers between devices: 11.3 us -> 16.8 us
    pallas_call x4 -> x6, Pallas kernels: 30.3 us -> 48.3 us  [the longest x2 31.5 us: code_stats(): pl.pallas_call(first_stats_kernel if first else second_stats_kernel, grid...]
    all_to_all x2 -> x3, waiting for transfers between devices: 30.6 us -> 22.8 us  [swap(): return lax.all_to_all(value, axis, split_axis=0, concat_axis=0, tiled=True)]
    all_to_all x2 -> x3, starting transfers between devices: 11.3 us -> 16.8 us  [swap(): return lax.all_to_all(value, axis, split_axis=0, concat_axis=0, tiled=True)]
    unnamed x6 -> x8, local copies, waits for them, and re-layouts: 4.56 us -> 4.37 us
  transfers between devices with their start and end apart: 2 -> 3, of which waited for: 2 -> 2; matrix products, arithmetic and copies ran while one was open for 1% -> 1% of each run, Pallas kernels for 2% -> 14%
where the time goes in v3:
time: 170 us; the launch traced here: 169 us
  blocking collectives  66.5 us (39%)
  Pallas kernels  53.8 us (32%)
  waiting for transfers between devices  22.8 us (13%)
  starting transfers between devices  16.8 us (10%)
  local copies, waits for them, and re-layouts  6.62 us (4%)
  other arithmetic  2.06 us (1%)
    all_to_all x5, blocking collectives, swap(): return lax.all_to_all(value, axis, split_axis=0, concat_axis=0, tiled=True)  66.5 us
    pallas_call x2, Pallas kernels, code_stats(): pl.pallas_call(first_stats_kernel if first else second_stats_kernel, grid...  31.5 us
    all_to_all x3, waiting for transfers between devices, swap(): return lax.all_to_all(value, axis, split_axis=0, concat_axis=0, tiled=True)  22.8 us
    all_to_all x3, starting transfers between devices, swap(): return lax.all_to_all(value, axis, split_axis=0, concat_axis=0, tiled=True)  16.8 us
    pallas_call x2, Pallas kernels, find_centres(): pl.pallas_call(partial(centres_kernel, half), out_shape=jax.ShapeDtypeStr...  11.5 us
    unnamed x8, local copies, waits for them, and re-layouts  4.37 us
    pallas_call x1, Pallas kernels, split_codes(): pl.pallas_call(codes_kernel, grid=(M // 4,), in_specs=[block(DSUB, K)], o...  3.79 us
  transfers between devices with their start and end apart: 3, of which 2 were waited for; matrix products, arithmetic and copies ran while one was open for 1% of the time, Pallas kernels for 14%

profile of v3, /device:TPU:1, one launch (start us, length us, event | category | flops | bytes accessed | tf_op | source)
XLA Modules:
  0.0 169.2 jit_solution(6623708456721943790)
XLA Ops:
  0.6 1.5 copy.9.owner_ref
  2.2 2.9 %slots.1 = (s32[1,512]{1,0:T(1,128)}, s32[1,512]{1,0:T(1,128)}, s32[8,128]{1,0:T(8,128)}) custom-call(s32[512,1]{1,0:T(8,128)} %copy.9.owner_ref, s32[1,512]{1,0:T(1,128)} %bitcast.23), custom_call_target="tpu_custom_call" | custom-call | tf_op jit(solution)/shard_map/slots/pallas_call | solution.py:222
  5.1 11.4 %all_to_all.46 = s32[8,1,128]{2,1,0:T(1,128)} all-to-all(s32[8,1,128]{2,1,0:T(1,128)} %bitcast.22), channel_id=1, replica_groups=mesh['x'=4,'c'=2,'z'=8,'y'=4] {'x','c'}, dimensions={0} | all-to-all | bytes 8192 | tf_op jit(solution)/shard_map/all_to_all | solution.py:290
  16.5 5.7 %centres.2 = bf16[8,64,1024]{2,1,0:T(8,128)(2,1)} custom-call(s32[8,128]{1,0:T(8,128)} %bitcast.20, bf16[1024,1024]{1,0:T(8,128)(2,1)} %centroids_ref.3), custom_call_target="tpu_custom_call" | custom-call | tf_op jit(solution)/shard_map/centres/pallas_call | solution.py:230
  22.3 4.3 %all-to-all-start.1 = ((bf16[8,64,1024]{2,1,0:T(8,128)(2,1)}), bf16[8,64,1024]{2,1,0:T(8,128)(2,1)S(1)}, u32[]{:S(2)}, u32[]{:S(2)}) async-start(bf16[8,64,1024]{2,1,0:T(8,128)(2,1)} %centres.2), calls=%async_computation.1 | async-start | bytes 2097152 | tf_op jit(solution)/shard_map/all_to_all | solution.py:290
  26.6 5.8 %centres.3 = bf16[8,64,1024]{2,1,0:T(8,128)(2,1)} custom-call(s32[8,128]{1,0:T(8,128)} %bitcast.21, bf16[1024,1024]{1,0:T(8,128)(2,1)} %centroids_ref.3), custom_call_target="tpu_custom_call" | custom-call | tf_op jit(solution)/shard_map/centres/pallas_call | solution.py:230
  32.3 9.4 %all-to-all-done.1 = bf16[8,64,1024]{2,1,0:T(8,128)(2,1)S(1)} async-done(((bf16[8,64,1024]{2,1,0:T(8,128)(2,1)}), bf16[8,64,1024]{2,1,0:T(8,128)(2,1)S(1)}, u32[]{:S(2)}, u32[]{:S(2)}) %all-to-all-start.1) | async-done | bytes 1048608 | tf_op jit(solution)/shard_map/all_to_all | solution.py:290
  41.7 0.0 copy-start
  41.7 4.3 %all-to-all-start.2 = ((bf16[8,64,1024]{2,1,0:T(8,128)(2,1)}), bf16[8,64,1024]{2,1,0:T(8,128)(2,1)S(1)}, u32[]{:S(2)}, u32[]{:S(2)}) async-start(bf16[8,64,1024]{2,1,0:T(8,128)(2,1)} %centres.3), calls=%async_computation.2 | async-start | bytes 2097152 | tf_op jit(solution)/shard_map/all_to_all | solution.py:290
  46.0 3.8 %codes.1 = (bf16[16,256,256]{2,1,0:T(8,128)(2,1)}, bf16[16,256,128]{2,1,0:T(8,128)(2,1)}, f32[16,1,256]{2,1,0:T(1,128)}) custom-call(f32[16,64,256]{2,1,0:T(8,128)} %book_ref.1), custom_call_target="tpu_custom_call" | custom-call | tf_op jit(solution)/shard_map/codes/pallas_call | solution.py:241
  49.8 0.0 copy-done
  49.8 14.1 %first_stats.1 = (f32[1024,384]{1,0:T(8,128)}, bf16[256,1024]{1,0:T(8,128)(2,1)}, bf16[1024,256]{1,0:T(8,128)(2,1)}) custom-call(bf16[512,1024]{1,0:T(8,128)(2,1)} %tokens_ref.3, s32[1,512]{1,0:T(1,128)} %get-tuple-element.13.rank_ref, s32[1,512]{1,0:T(1,128)} %get-tuple-element.14.slot_ref, bf16[512,1024]{1,0:T(8,128)(2,1)} %bitcast.13, ...), custom_call_target="tpu_custom_call" | custom-call | tf_op jit(solution)/shard_map/first_stats/pallas_call | solution.py:268
  63.9 0.0 all-to-all-done.2
  63.9 0.0 copy-start.1
  63.9 1.1 copy-done.1
  64.9 17.5 %second_stats.1 = bf16[1024,1408]{1,0:T(8,128)(2,1)} custom-call(bf16[512,1024]{1,0:T(8,128)(2,1)} %tokens_ref.3, s32[1,512]{1,0:T(1,128)} %get-tuple-element.13.rank_ref, s32[1,512]{1,0:T(1,128)} %get-tuple-element.14.slot_ref, bf16[512,1024]{1,0:T(8,128)(2,1)} %bitcast.14, bf16[512,1024]{1,0:T(8,128)(2,1)} %bitcast.16, bf16[1024,1024]{1,0:T(8,128)(2,1)} %rotation_ref.3, ...), custom_call_target="tpu_custom_call" | custom-call | tf_op jit(solution)/shard_map/second_stats/pallas_call | solution.py:268
  82.4 7.2 %all_to_all.47 = bf16[2,512,1408]{2,1,0:T(8,128)(2,1)S(1)} all-to-all(bf16[2,512,1408]{2,1,0:T(8,128)(2,1)} %bitcast.12), channel_id=1, replica_groups=mesh['x'=4,'c'=2,'z'=8,'y'=4] {'c'}, dimensions={0} | all-to-all | bytes 5767168 | tf_op jit(solution)/shard_map/all_to_all | solution.py:290
  89.6 2.1 %reduce_sum.12 = bf16[512,1408]{1,0:T(8,128)(2,1)} reduce(bf16[2,512,1408]{2,1,0:T(8,128)(2,1)S(1)} %all_to_all.47, bf16[]{:T(256)} %constant.10.clone.1), dimensions={0}, to_apply=%region_0.0 | reduce | flops 720896 | bytes 4325378 | tf_op jit(solution)/shard_map/reduce_sum | solution.py:307
  91.7 25.6 %all_to_all.48.part_ref = bf16[16,32,1408]{2,1,0:T(8,128)(2,1)} all-to-all(bf16[16,32,1408]{2,1,0:T(8,128)(2,1)} %bitcast.15), channel_id=1, replica_groups=mesh['x'=4,'c'=2,'z'=8,'y'=4] {'x','y'}, dimensions={0} | all-to-all | bytes 2883584 | tf_op jit(solution)/shard_map/all_to_all | solution.py:290
  117.3 2.3 %pack.1 = f32[8,16,1024]{2,1,0:T(8,128)} custom-call(bf16[16,32,1408]{2,1,0:T(8,128)(2,1)} %all_to_all.48.part_ref), custom_call_target="tpu_custom_call" | custom-call | tf_op jit(solution)/shard_map/pack/pallas_call | solution.py:203
  119.6 8.2 %all-to-all-start.5 = ((f32[8,16,1024]{2,1,0:T(8,128)}), f32[8,16,1024]{2,1,0:T(8,128)S(1)}, u32[]{:S(2)}, u32[]{:S(2)}) async-start(f32[8,16,1024]{2,1,0:T(8,128)} %pack.1), calls=%async_computation.5 | async-start | bytes 1048576 | tf_op jit(solution)/shard_map/all_to_all | solution.py:290
  127.8 1.4 constant_dynamic-slice_fusion.book_ref
  129.2 13.5 %all-to-all-done.5.part_ref = f32[8,16,1024]{2,1,0:T(8,128)S(1)} async-done(((f32[8,16,1024]{2,1,0:T(8,128)}), f32[8,16,1024]{2,1,0:T(8,128)S(1)}, u32[]{:S(2)}, u32[]{:S(2)}) %all-to-all-start.5) | async-done | bytes 524320 | tf_op jit(solution)/shard_map/all_to_all | solution.py:290
  142.7 0.0 copy-start.2
  142.7 0.8 copy-done.2
  143.5 1.7 finish.1
  145.2 0.8 broadcast_in_dim.6
  146.0 14.1 %all_to_all.49 = f32[16,32,256]{2,1,0:T(8,128)S(1)} all-to-all(f32[16,32,256]{2,1,0:T(8,128)S(1)} %broadcast_in_dim.6), channel_id=1, replica_groups=mesh['x'=4,'c'=2,'z'=8,'y'=4] {'x','y'}, dimensions={0} | all-to-all | bytes 1048576 | tf_op jit(solution)/shard_map/all_to_all | solution.py:290
  160.1 0.1 broadcast_in_dim.7
  160.2 8.1 %all_to_all.50 = f32[2,512,256]{2,1,0:T(8,128)S(1)} all-to-all(f32[2,512,256]{2,1,0:T(8,128)S(1)} %broadcast_in_dim.7), channel_id=1, replica_groups=mesh['x'=4,'c'=2,'z'=8,'y'=4] {'c'}, dimensions={0} | all-to-all | bytes 2097152 | tf_op jit(solution)/shard_map/all_to_all | solution.py:290
  168.3 1.0 copy.12
Async XLA Ops:
  22.3 19.4 %all-to-all-start.1 = ((bf16[8,64,1024]{2,1,0:T(8,128)(2,1)}), bf16[8,64,1024]{2,1,0:T(8,128)(2,1)S(1)}, u32[]{:S(2)}, u32[]{:S(2)}) async-start(bf16[8,64,1024]{2,1,0:T(8,128)(2,1)} %centres.2), calls=%async_computation.1 | async-start | bytes 2097152 | tf_op jit(solution)/shard_map/all_to_all | solution.py:290
  41.7 8.1 %copy-start = (bf16[8,64,1024]{2,1,0:T(8,128)(2,1)}, bf16[8,64,1024]{2,1,0:T(8,128)(2,1)S(1)}, u32[]{:S(2)}) copy-start(bf16[8,64,1024]{2,1,0:T(8,128)(2,1)S(1)} %all-to-all-done.1) | copy-start | bytes 3145732
  41.7 22.2 %all-to-all-start.2 = ((bf16[8,64,1024]{2,1,0:T(8,128)(2,1)}), bf16[8,64,1024]{2,1,0:T(8,128)(2,1)S(1)}, u32[]{:S(2)}, u32[]{:S(2)}) async-start(bf16[8,64,1024]{2,1,0:T(8,128)(2,1)} %centres.3), calls=%async_computation.2 | async-start | bytes 2097152 | tf_op jit(solution)/shard_map/all_to_all | solution.py:290
  63.9 1.1 copy-start.1
  119.6 23.1 %all-to-all-start.5 = ((f32[8,16,1024]{2,1,0:T(8,128)}), f32[8,16,1024]{2,1,0:T(8,128)S(1)}, u32[]{:S(2)}, u32[]{:S(2)}) async-start(f32[8,16,1024]{2,1,0:T(8,128)} %pack.1), calls=%async_computation.5 | async-start | bytes 1048576 | tf_op jit(solution)/shard_map/all_to_all | solution.py:290
  142.7 0.8 copy-start.2

commit v4 on v2

--- a/solution.py
+++ b/solution.py
@@ -38,7 +38,7 @@
 
 
 def slots_kernel(owner_ref, lists_ref, slot_ref, ids_ref):
-    owner = owner_ref[...]
+    owner = jnp.broadcast_to(owner_ref[...].astype(F32), (128, ROWS)).T[:, 0:1].astype(jnp.int32)
     mine = owner == iota((ROWS, 128), 1)
     earlier = one_hot(iota((ROWS, ROWS), 0) > iota((ROWS, ROWS), 1))
     before = dot(earlier, one_hot(mine))
@@ -54,12 +54,15 @@
         ids_ref[o : o + 1, :] = ids[:, o * CAP : (o + 1) * CAP].astype(jnp.int32)
 
 
-def centres_kernel(ids_ref, centroids_ref, out_ref):
-    ids = ids_ref[...].astype(F32).T.astype(jnp.int32)
-    table = centroids_ref[...]
-    for s in range(OWNERS):
-        pick = one_hot(ids[:, s : s + 1] == iota((CAP, LISTS), 1))
-        out_ref[s] = dot(pick, table).astype(BF16)
+def centres_kernel(ids_ref, centroids_ref, out_ref, pick_ref):
+    @pl.when(pl.program_id(0) == 0)
+    def _():
+        ids = ids_ref[...].astype(F32).T.astype(jnp.int32)
+        for s in range(OWNERS):
+            at = slice(s * CAP, (s + 1) * CAP)
+            pick_ref[at] = one_hot(ids[:, s : s + 1] == iota((CAP, LISTS), 1))
+
+    out_ref[...] = dot(pick_ref[...], centroids_ref[...]).astype(BF16)
 
 
 def codes_kernel(book_ref, stack_ref, turned_ref, norm_ref):
@@ -85,11 +88,7 @@
         centres = dot(pick, got_ref[...])
         res = (tokens_ref[...].astype(F32) - centres).astype(BF16)
         res_ref[...] = res
-        d = iota((D, D), 1)
-        place = (
-            ((d >> 7) & 1) * 512 + (d >> 8) * 128 + ((d >> 2) & 3) * 32 + ((d >> 4) & 7) * 4
-        ) + (d & 3)
-        turned_res_ref[...] = dot(one_hot(iota((D, D), 0) == place), res, 1, 1).astype(BF16)
+        turned_res_ref[...] = res.T
 
     rotated = dot(res_ref[...], rotation_ref[...])
     left = iota((ROWS, 2 * DSUB), 1) < DSUB
@@ -123,7 +122,18 @@
     for q in range(4):
         @pl.when(step == q)
         def _():
-            out_ref[:, q * 256 : (q + 1) * 256] = cross
+            for block in range(8):
+                at = (block % 2) * 512 + (block // 2) * 128
+                piece = cross[block * 128 : block * 128 + 128]
+                out_ref[at : at + 128, q * 256 : (q + 1) * 256] = piece
+
+
+def add_kernel(pair_ref, out_ref):
+    total = (pair_ref[0].astype(F32) + pair_ref[1].astype(F32)).astype(BF16)
+    w = iota((128, 128), 1)
+    place = ((w >> 2) & 3) * 32 + (w >> 4) * 4 + (w & 3)
+    out_ref[:, :D] = dot(one_hot(iota((128, 128), 0) == place), total[:, :D]).astype(BF16)
+    out_ref[:, D:] = total[:, D:]
 
 
 def pack_kernel(part_ref, out_ref):
@@ -131,7 +141,8 @@
     for i in range(1, 16):
         total = total + part_ref[i].astype(F32)
     mass = jnp.concatenate([total[0:1, D + K :], total[1:2, D + K :], jnp.zeros((1, D - K), F32)], axis=1)
-    mass = jnp.broadcast_to(mass, (4, D))
+    high = mass.astype(BF16).astype(F32)
+    mass = jnp.where(iota((4, D), 0) == 0, high, jnp.where(iota((4, D), 0) == 1, mass - high, 0.0))
     num = jnp.concatenate([total[8 * b : 8 * b + 8, D : D + K] for b in range(4)], axis=1)
     for z in range(8):
         head = jnp.concatenate([total[4 * z : 4 * z + 4, :D], mass], axis=0)
@@ -143,10 +154,21 @@
     for i in range(1, 8):
         total = total + part_ref[i].astype(F32)
     cross_ref[...] = total[0:4] * (1.0 / math.sqrt(ROWS * 256))
-    count = total[4:5, :K] + 1.0
+    count = total[4:5, :K] + total[5:6, :K] + 1.0
     for b in range(4):
         at = slice(8 * b, 8 * b + 8)
         fresh_ref[at] = (total[8:16, b * K : (b + 1) * K] + book_ref[at]) / count
+
+
+def add(pair):
+    return pl.pallas_call(
+        add_kernel,
+        grid=(4,),
+        in_specs=[pl.BlockSpec((2, 128, WIDE), lambda i: (0, i, 0))],
+        out_specs=pl.BlockSpec((128, WIDE), lambda i: (i, 0)),
+        out_shape=jax.ShapeDtypeStruct((512, WIDE), BF16),
+        name="add",
+    )(pair)
 
 
 def pack(part):
@@ -175,15 +197,20 @@
             jax.ShapeDtypeStruct((OWNERS, CAP), jnp.int32),
         ),
         name="slots",
-    )(owner, lists.reshape(1, ROWS))
+    )(owner.reshape(1, ROWS), lists.reshape(1, ROWS))
 
 
 def find_centres(ids, centroids):
+    columns = pl.BlockSpec((LISTS, 256), lambda i: (0, i))
     return pl.pallas_call(
         centres_kernel,
-        out_shape=jax.ShapeDtypeStruct((OWNERS, CAP, D), BF16),
+        grid=(D // 256,),
+        in_specs=[whole((OWNERS, CAP)), columns],
+        out_specs=columns,
+        out_shape=jax.ShapeDtypeStruct((OWNERS * CAP, D), BF16),
+        scratch_shapes=[pltpu.VMEM((OWNERS * CAP, LISTS), BF16)],
         name="centres",
-    )(ids, centroids)
+    )(ids, centroids).reshape(OWNERS, CAP, D)
 
 
 def split_codes(codebook):
@@ -241,7 +268,7 @@
     centres = find_centres(swap(ids, GRP), centroids)
     got = swap(centres, GRP).reshape(OWNERS * CAP, D)
     part = code_stats(tokens, slot, got, rotation, split_codes(codebook))
-    part = swap(part.reshape(2, 512, WIDE), "c").astype(F32).sum(axis=0).astype(BF16)
+    part = add(swap(part.reshape(2, 512, WIDE), "c"))
     part = swap(pack(swap(part.reshape(16, 32, WIDE), XY)), "z")
     place = lax.axis_index("c") * 16 + lax.axis_index(XY)
     book = lax.dynamic_slice_in_dim(codebook.reshape(M * DSUB, K), place * 32, 32, 0)

time: 154 us -> 156 us (1.013)
  Pallas kernels: 35.7 us -> 39 us
  blocking collectives: 66 us -> 68.6 us
  other arithmetic: 2.05 us -> 0 us
    pallas_call x1 -> x2, Pallas kernels: 5.42 us -> 10 us  [the longest x1 5.79 us: find_centres(): pl.pallas_call(centres_kernel, grid=(D // 256,), in_specs=[whole((OWNERS,...]
    all_to_all x5, blocking collectives: 66 us -> 68.6 us  [swap(): return lax.all_to_all(value, axis, split_axis=0, concat_axis=0, tiled=True)]
    reduce_sum x1 -> x0, other arithmetic: 2.05 us -> none  [local(): swap(part.reshape(2, 512, WIDE), 'c').astype(F32).sum(axis=0).astype(BF16)]
    unnamed x6 -> x5, local copies, waits for them, and re-layouts: 4.56 us -> 3.03 us
where the time goes in v4:
time: 156 us; the launch traced here: 155 us
  blocking collectives  68.6 us (44%)
  Pallas kernels  39 us (25%)
  waiting for transfers between devices  30.6 us (20%)
  starting transfers between devices  11.3 us (7%)
  local copies, waits for them, and re-layouts  5.26 us (3%)
    all_to_all x5, blocking collectives, swap(): return lax.all_to_all(value, axis, split_axis=0, concat_axis=0, tiled=True)  68.6 us
    all_to_all x2, waiting for transfers between devices, swap(): return lax.all_to_all(value, axis, split_axis=0, concat_axis=0, tiled=True)  30.6 us
    pallas_call x1, Pallas kernels, code_stats(): pl.pallas_call(stats_kernel, grid=(M // 4,), in_specs=[whole((ROWS, D)),...  18.7 us
    all_to_all x2, starting transfers between devices, swap(): return lax.all_to_all(value, axis, split_axis=0, concat_axis=0, tiled=True)  11.3 us
    pallas_call x1, Pallas kernels, find_centres(): pl.pallas_call(centres_kernel, grid=(D // 256,), in_specs=[whole((OWNERS,...  5.79 us
    pallas_call x1, Pallas kernels, add(): pl.pallas_call(add_kernel, grid=(4,), in_specs=[pl.BlockSpec((2, 128, WID...  4.24 us
    pallas_call x1, Pallas kernels, split_codes(): pl.pallas_call(codes_kernel, grid=(M // 4,), in_specs=[block(DSUB, K)], o...  3.79 us
  transfers between devices with their start and end apart: 2, of which 2 were waited for; matrix products, arithmetic and copies ran while one was open for 1% of the time, Pallas kernels for 2%

profile of v4, /device:TPU:1, one launch (start us, length us, event | category | flops | bytes accessed | tf_op | source)
XLA Modules:
  0.0 155.5 jit_solution(16594534763508474873)
XLA Ops:
  0.6 2.7 %slots.1 = (s32[512,1]{1,0:T(8,128)}, s32[8,128]{1,0:T(8,128)}) custom-call(s32[1,512]{1,0:T(1,128)} %bitcast.22, s32[1,512]{1,0:T(1,128)} %bitcast.23), custom_call_target="tpu_custom_call" | custom-call | tf_op jit(solution)/shard_map/slots/pallas_call | solution.py:193
  3.3 11.5 %all_to_all.41 = s32[8,1,128]{2,1,0:T(1,128)} all-to-all(s32[8,1,128]{2,1,0:T(1,128)} %bitcast.21), channel_id=1, replica_groups=mesh['x'=4,'c'=2,'z'=8,'y'=4] {'x','c'}, dimensions={0} | all-to-all | bytes 8192 | tf_op jit(solution)/shard_map/all_to_all | solution.py:258
  14.8 5.8 %centres.1 = bf16[1024,1024]{1,0:T(8,128)(2,1)} custom-call(s32[8,128]{1,0:T(8,128)} %bitcast.20, bf16[1024,1024]{1,0:T(8,128)(2,1)} %centroids_ref.1), custom_call_target="tpu_custom_call" | custom-call | tf_op jit(solution)/shard_map/centres/pallas_call | solution.py:205
  20.6 4.4 %all-to-all-start.1 = ((bf16[8,128,1024]{2,1,0:T(8,128)(2,1)}), bf16[8,128,1024]{2,1,0:T(8,128)(2,1)S(1)}, u32[]{:S(2)}, u32[]{:S(2)}) async-start(bf16[8,128,1024]{2,1,0:T(8,128)(2,1)} %bitcast.14), calls=%async_computation.1 | async-start | bytes 4194304 | tf_op jit(solution)/shard_map/all_to_all | solution.py:258
  24.9 3.8 %codes.1 = (bf16[16,256,256]{2,1,0:T(8,128)(2,1)}, bf16[16,256,128]{2,1,0:T(8,128)(2,1)}, f32[16,1,256]{2,1,0:T(1,128)}) custom-call(f32[16,64,256]{2,1,0:T(8,128)} %book_ref.1), custom_call_target="tpu_custom_call" | custom-call | tf_op jit(solution)/shard_map/codes/pallas_call | solution.py:220
  28.7 22.6 %all-to-all-done.1 = bf16[8,128,1024]{2,1,0:T(8,128)(2,1)S(1)} async-done(((bf16[8,128,1024]{2,1,0:T(8,128)(2,1)}), bf16[8,128,1024]{2,1,0:T(8,128)(2,1)S(1)}, u32[]{:S(2)}, u32[]{:S(2)}) %all-to-all-start.1) | async-done | bytes 2097184 | tf_op jit(solution)/shard_map/all_to_all | solution.py:258
  51.3 0.0 copy-start
  51.3 1.4 copy-done
  52.6 18.7 %stats.1 = bf16[1024,1408]{1,0:T(8,128)(2,1)} custom-call(bf16[512,1024]{1,0:T(8,128)(2,1)} %tokens_ref.1, s32[512,1]{1,0:T(8,128)} %get-tuple-element.9.slot_ref, bf16[1024,1024]{1,0:T(8,128)(2,1)} %bitcast.15, bf16[1024,1024]{1,0:T(8,128)(2,1)} %rotation_ref.1, bf16[16,256,256]{2,1,0:T(8,128)(2,1)} %get-tuple-element.11.stack_ref, ...), custom_call_target="tpu_custom_call" | custom-call | tf_op jit(solution)/shard_map/stats/pallas_call | solution.py:238
  71.3 10.4 %all_to_all.42.pair_ref = bf16[2,512,1408]{2,1,0:T(8,128)(2,1)} all-to-all(bf16[2,512,1408]{2,1,0:T(8,128)(2,1)} %bitcast.13), channel_id=1, replica_groups=mesh['x'=4,'c'=2,'z'=8,'y'=4] {'c'}, dimensions={0} | all-to-all | bytes 5767168 | tf_op jit(solution)/shard_map/all_to_all | solution.py:258
  81.7 4.2 %add.13 = bf16[512,1408]{1,0:T(8,128)(2,1)} custom-call(bf16[2,512,1408]{2,1,0:T(8,128)(2,1)} %all_to_all.42.pair_ref), custom_call_target="tpu_custom_call" | custom-call | tf_op jit(solution)/shard_map/add/pallas_call | solution.py:164
  85.9 24.7 %all_to_all.43.part_ref = bf16[16,32,1408]{2,1,0:T(8,128)(2,1)} all-to-all(bf16[16,32,1408]{2,1,0:T(8,128)(2,1)} %bitcast.16), channel_id=1, replica_groups=mesh['x'=4,'c'=2,'z'=8,'y'=4] {'x','y'}, dimensions={0} | all-to-all | bytes 2883584 | tf_op jit(solution)/shard_map/all_to_all | solution.py:258
  110.7 2.3 %pack.1 = bf16[8,16,1024]{2,1,0:T(8,128)(2,1)} custom-call(bf16[16,32,1408]{2,1,0:T(8,128)(2,1)} %all_to_all.43.part_ref), custom_call_target="tpu_custom_call" | custom-call | tf_op jit(solution)/shard_map/pack/pallas_call | solution.py:175
  112.9 6.9 %all-to-all-start.4 = ((bf16[8,16,1024]{2,1,0:T(8,128)(2,1)}), bf16[8,16,1024]{2,1,0:T(8,128)(2,1)S(1)}, u32[]{:S(2)}, u32[]{:S(2)}) async-start(bf16[8,16,1024]{2,1,0:T(8,128)(2,1)} %pack.1), calls=%async_computation.4 | async-start | bytes 524288 | tf_op jit(solution)/shard_map/all_to_all | solution.py:258
  119.9 1.4 constant_dynamic-slice_fusion.book_ref
  121.2 8.0 %all-to-all-done.4.part_ref = bf16[8,16,1024]{2,1,0:T(8,128)(2,1)S(1)} async-done(((bf16[8,16,1024]{2,1,0:T(8,128)(2,1)}), bf16[8,16,1024]{2,1,0:T(8,128)(2,1)S(1)}, u32[]{:S(2)}, u32[]{:S(2)}) %all-to-all-start.4) | async-done | bytes 262176 | tf_op jit(solution)/shard_map/all_to_all | solution.py:258
  129.3 0.0 copy-start.1
  129.3 0.7 copy-done.1
  130.0 1.6 %finish.1 = (f32[4,1024]{1,0:T(4,128)}, f32[32,256]{1,0:T(8,128)}) custom-call(bf16[8,16,1024]{2,1,0:T(8,128)(2,1)} %copy-done.1, f32[32,256]{1,0:T(8,128)} %constant_dynamic-slice_fusion.book_ref), custom_call_target="tpu_custom_call" | custom-call | tf_op jit(solution)/shard_map/finish/pallas_call | solution.py:181
  131.6 0.8 broadcast_in_dim.6
  132.4 13.1 %all_to_all.44 = f32[16,32,256]{2,1,0:T(8,128)S(1)} all-to-all(f32[16,32,256]{2,1,0:T(8,128)S(1)} %broadcast_in_dim.6), channel_id=1, replica_groups=mesh['x'=4,'c'=2,'z'=8,'y'=4] {'x','y'}, dimensions={0} | all-to-all | bytes 1048576 | tf_op jit(solution)/shard_map/all_to_all | solution.py:258
  145.4 0.1 broadcast_in_dim.7
  145.5 9.0 %all_to_all.45 = f32[2,512,256]{2,1,0:T(8,128)S(1)} all-to-all(f32[2,512,256]{2,1,0:T(8,128)S(1)} %broadcast_in_dim.7), channel_id=1, replica_groups=mesh['x'=4,'c'=2,'z'=8,'y'=4] {'c'}, dimensions={0} | all-to-all | bytes 2097152 | tf_op jit(solution)/shard_map/all_to_all | solution.py:258
  154.5 1.0 copy.10
Async XLA Ops:
  20.6 30.7 %all-to-all-start.1 = ((bf16[8,128,1024]{2,1,0:T(8,128)(2,1)}), bf16[8,128,1024]{2,1,0:T(8,128)(2,1)S(1)}, u32[]{:S(2)}, u32[]{:S(2)}) async-start(bf16[8,128,1024]{2,1,0:T(8,128)(2,1)} %bitcast.14), calls=%async_computation.1 | async-start | bytes 4194304 | tf_op jit(solution)/shard_map/all_to_all | solution.py:258
  51.3 1.4 copy-start
  112.9 16.3 %all-to-all-start.4 = ((bf16[8,16,1024]{2,1,0:T(8,128)(2,1)}), bf16[8,16,1024]{2,1,0:T(8,128)(2,1)S(1)}, u32[]{:S(2)}, u32[]{:S(2)}) async-start(bf16[8,16,1024]{2,1,0:T(8,128)(2,1)} %pack.1), calls=%async_computation.4 | async-start | bytes 524288 | tf_op jit(solution)/shard_map/all_to_all | solution.py:258
  129.3 0.7 copy-start.1

commit v5 on v4

--- a/solution.py
+++ b/solution.py
@@ -88,7 +88,11 @@
         centres = dot(pick, got_ref[...])
         res = (tokens_ref[...].astype(F32) - centres).astype(BF16)
         res_ref[...] = res
-        turned_res_ref[...] = res.T
+        d = iota((D, D), 1)
+        place = (
+            ((d >> 7) & 1) * 512 + (d >> 8) * 128 + ((d >> 2) & 3) * 32 + ((d >> 4) & 7) * 4
+        ) + (d & 3)
+        turned_res_ref[...] = dot(one_hot(iota((D, D), 0) == place), res, 1, 1).astype(BF16)
 
     rotated = dot(res_ref[...], rotation_ref[...])
     left = iota((ROWS, 2 * DSUB), 1) < DSUB
@@ -122,24 +126,11 @@
     for q in range(4):
         @pl.when(step == q)
         def _():
-            for block in range(8):
-                at = (block % 2) * 512 + (block // 2) * 128
-                piece = cross[block * 128 : block * 128 + 128]
-                out_ref[at : at + 128, q * 256 : (q + 1) * 256] = piece
-
-
-def add_kernel(pair_ref, out_ref):
-    total = (pair_ref[0].astype(F32) + pair_ref[1].astype(F32)).astype(BF16)
-    w = iota((128, 128), 1)
-    place = ((w >> 2) & 3) * 32 + (w >> 4) * 4 + (w & 3)
-    out_ref[:, :D] = dot(one_hot(iota((128, 128), 0) == place), total[:, :D]).astype(BF16)
-    out_ref[:, D:] = total[:, D:]
+            out_ref[:, q * 256 : (q + 1) * 256] = cross
 
 
 def pack_kernel(part_ref, out_ref):
-    total = part_ref[0].astype(F32)
-    for i in range(1, 16):
-        total = total + part_ref[i].astype(F32)
+    total = part_ref[...]
     mass = jnp.concatenate([total[0:1, D + K :], total[1:2, D + K :], jnp.zeros((1, D - K), F32)], axis=1)
     high = mass.astype(BF16).astype(F32)
     mass = jnp.where(iota((4, D), 0) == 0, high, jnp.where(iota((4, D), 0) == 1, mass - high, 0.0))
@@ -149,40 +140,10 @@
         out_ref[z] = jnp.concatenate([head, num], axis=0).astype(BF16)
 
 
-def finish_kernel(part_ref, book_ref, cross_ref, fresh_ref):
-    total = part_ref[0].astype(F32)
-    for i in range(1, 8):
-        total = total + part_ref[i].astype(F32)
-    cross_ref[...] = total[0:4] * (1.0 / math.sqrt(ROWS * 256))
-    count = total[4:5, :K] + total[5:6, :K] + 1.0
-    for b in range(4):
-        at = slice(8 * b, 8 * b + 8)
-        fresh_ref[at] = (total[8:16, b * K : (b + 1) * K] + book_ref[at]) / count
-
-
-def add(pair):
-    return pl.pallas_call(
-        add_kernel,
-        grid=(4,),
-        in_specs=[pl.BlockSpec((2, 128, WIDE), lambda i: (0, i, 0))],
-        out_specs=pl.BlockSpec((128, WIDE), lambda i: (i, 0)),
-        out_shape=jax.ShapeDtypeStruct((512, WIDE), BF16),
-        name="add",
-    )(pair)
-
-
 def pack(part):
     return pl.pallas_call(
         pack_kernel, out_shape=jax.ShapeDtypeStruct((8, 16, D), BF16), name="pack"
     )(part)
-
-
-def finish(part, book):
-    return pl.pallas_call(
-        finish_kernel,
-        out_shape=(jax.ShapeDtypeStruct((4, D), F32), jax.ShapeDtypeStruct((32, K), F32)),
-        name="finish",
-    )(part, book)
 
 
 def whole(shape):
@@ -268,11 +229,14 @@
     centres = find_centres(swap(ids, GRP), centroids)
     got = swap(centres, GRP).reshape(OWNERS * CAP, D)
     part = code_stats(tokens, slot, got, rotation, split_codes(codebook))
-    part = add(swap(part.reshape(2, 512, WIDE), "c"))
-    part = swap(pack(swap(part.reshape(16, 32, WIDE), XY)), "z")
+    part = swap(part.reshape(2, 512, WIDE), "c").astype(F32).sum(axis=0).astype(BF16)
+    part = swap(part.reshape(16, 32, WIDE), XY).astype(F32).sum(axis=0)
+    part = swap(pack(part), "z").astype(F32).sum(axis=0)
+    cross_cov = part[:4] * (1.0 / math.sqrt(ROWS * 256))
     place = lax.axis_index("c") * 16 + lax.axis_index(XY)
     book = lax.dynamic_slice_in_dim(codebook.reshape(M * DSUB, K), place * 32, 32, 0)
-    cross_cov, fresh = finish(part, book)
+    num = jnp.concatenate([part[8:, b * K : (b + 1) * K] for b in range(4)], axis=0)
+    fresh = (num + book) / (part[4:5, :K] + part[5:6, :K] + 1.0)
     fresh = sent_to_all(sent_to_all(fresh, XY), "c")
     return (fresh.reshape(M, DSUB, K), cross_cov)
 

time: 156 us -> 151 us (0.968)
  blocking collectives: 68.6 us -> 51.8 us
  waiting for transfers between devices: 30.6 us -> 40.3 us
  Pallas kernels: 39 us -> 33.6 us
  starting transfers between devices: 11.3 us -> 16.5 us
  other arithmetic: 0 us -> 4.34 us
  local copies, waits for them, and re-layouts: 5.26 us -> 3.25 us
    all_to_all x5 -> x4, blocking collectives: 68.6 us -> 51.8 us  [swap(): return lax.all_to_all(value, axis, split_axis=0, concat_axis=0, tiled=True)]
    all_to_all x2 -> x3, waiting for transfers between devices: 30.6 us -> 40.3 us  [swap(): return lax.all_to_all(value, axis, split_axis=0, concat_axis=0, tiled=True)]
    pallas_call x2 -> x0, Pallas kernels: 5.85 us -> none  [the longest x1 4.24 us: add(): pl.pallas_call(add_kernel, grid=(4,), in_specs=[pl.BlockSpec((2, 128, WID...]
    all_to_all x2 -> x3, starting transfers between devices: 11.3 us -> 16.5 us  [swap(): return lax.all_to_all(value, axis, split_axis=0, concat_axis=0, tiled=True)]
    reduce_sum x0 -> x3, other arithmetic: none -> 2.95 us  [the longest x1 2.05 us: local(): swap(part.reshape(2, 512, WIDE), 'c').astype(F32).sum(axis=0).astype(BF16)]
  transfers between devices with their start and end apart: 2 -> 3, of which waited for: 2 -> 3; matrix products, arithmetic and copies ran while one was open for 1% -> 0% of each run, Pallas kernels for 2% -> 3%
where the time goes in v5:
time: 151 us; the launch traced here: 150 us
  blocking collectives  51.8 us (34%)
  waiting for transfers between devices  40.3 us (27%)
  Pallas kernels  33.6 us (22%)
  starting transfers between devices  16.5 us (11%)
  other arithmetic  4.34 us (3%)
  local copies, waits for them, and re-layouts  3.25 us (2%)
    all_to_all x4, blocking collectives, swap(): return lax.all_to_all(value, axis, split_axis=0, concat_axis=0, tiled=True)  51.8 us
    all_to_all x3, waiting for transfers between devices, swap(): return lax.all_to_all(value, axis, split_axis=0, concat_axis=0, tiled=True)  40.3 us
    pallas_call x1, Pallas kernels, code_stats(): pl.pallas_call(stats_kernel, grid=(M // 4,), in_specs=[whole((ROWS, D)),...  19.7 us
    all_to_all x3, starting transfers between devices, swap(): return lax.all_to_all(value, axis, split_axis=0, concat_axis=0, tiled=True)  16.5 us
    pallas_call x1, Pallas kernels, find_centres(): pl.pallas_call(centres_kernel, grid=(D // 256,), in_specs=[whole((OWNERS,...  5.8 us
    pallas_call x1, Pallas kernels, split_codes(): pl.pallas_call(codes_kernel, grid=(M // 4,), in_specs=[block(DSUB, K)], o...  3.79 us
  transfers between devices with their start and end apart: 3, of which 3 were waited for; matrix products, arithmetic and copies ran while one was open for 0% of the time, Pallas kernels for 3%

profile of v5, /device:TPU:1, one launch (start us, length us, event | category | flops | bytes accessed | tf_op | source)
XLA Modules:
  0.0 150.5 jit_solution(9919707641288008673)
XLA Ops:
  0.6 2.7 %slots.1 = (s32[512,1]{1,0:T(8,128)}, s32[8,128]{1,0:T(8,128)}) custom-call(s32[1,512]{1,0:T(1,128)} %bitcast.24, s32[1,512]{1,0:T(1,128)} %bitcast.25), custom_call_target="tpu_custom_call" | custom-call | tf_op jit(solution)/shard_map/slots/pallas_call | solution.py:154
  3.3 11.6 %all_to_all.41 = s32[8,1,128]{2,1,0:T(1,128)} all-to-all(s32[8,1,128]{2,1,0:T(1,128)} %bitcast.23), channel_id=1, replica_groups=mesh['x'=4,'c'=2,'z'=8,'y'=4] {'x','c'}, dimensions={0} | all-to-all | bytes 8192 | tf_op jit(solution)/shard_map/all_to_all | solution.py:219
  14.9 5.8 %centres.1 = bf16[1024,1024]{1,0:T(8,128)(2,1)} custom-call(s32[8,128]{1,0:T(8,128)} %bitcast.21, bf16[1024,1024]{1,0:T(8,128)(2,1)} %centroids_ref.1), custom_call_target="tpu_custom_call" | custom-call | tf_op jit(solution)/shard_map/centres/pallas_call | solution.py:166
  20.7 4.0 %all-to-all-start.1 = ((bf16[8,128,1024]{2,1,0:T(8,128)(2,1)}), bf16[8,128,1024]{2,1,0:T(8,128)(2,1)S(1)}, u32[]{:S(2)}, u32[]{:S(2)}) async-start(bf16[8,128,1024]{2,1,0:T(8,128)(2,1)} %bitcast.15), calls=%async_computation.1 | async-start | bytes 4194304 | tf_op jit(solution)/shard_map/all_to_all | solution.py:219
  24.7 3.8 %codes.1 = (bf16[16,256,256]{2,1,0:T(8,128)(2,1)}, bf16[16,256,128]{2,1,0:T(8,128)(2,1)}, f32[16,1,256]{2,1,0:T(1,128)}) custom-call(f32[16,64,256]{2,1,0:T(8,128)} %book_ref.1), custom_call_target="tpu_custom_call" | custom-call | tf_op jit(solution)/shard_map/codes/pallas_call | solution.py:181
  28.5 22.6 %all-to-all-done.1 = bf16[8,128,1024]{2,1,0:T(8,128)(2,1)S(1)} async-done(((bf16[8,128,1024]{2,1,0:T(8,128)(2,1)}), bf16[8,128,1024]{2,1,0:T(8,128)(2,1)S(1)}, u32[]{:S(2)}, u32[]{:S(2)}) %all-to-all-start.1) | async-done | bytes 2097184 | tf_op jit(solution)/shard_map/all_to_all | solution.py:219
  51.1 0.0 copy-start
  51.1 1.4 copy-done
  52.4 19.7 %stats.1 = bf16[1024,1408]{1,0:T(8,128)(2,1)} custom-call(bf16[512,1024]{1,0:T(8,128)(2,1)} %tokens_ref.1, s32[512,1]{1,0:T(8,128)} %get-tuple-element.7.slot_ref, bf16[1024,1024]{1,0:T(8,128)(2,1)} %bitcast.16, bf16[1024,1024]{1,0:T(8,128)(2,1)} %rotation_ref.1, bf16[16,256,256]{2,1,0:T(8,128)(2,1)} %get-tuple-element.9.stack_ref, ...), custom_call_target="tpu_custom_call" | custom-call | tf_op jit(solution)/shard_map/stats/pallas_call | solution.py:199
  72.1 7.8 %all_to_all.42 = bf16[2,512,1408]{2,1,0:T(8,128)(2,1)S(1)} all-to-all(bf16[2,512,1408]{2,1,0:T(8,128)(2,1)} %bitcast.14), channel_id=1, replica_groups=mesh['x'=4,'c'=2,'z'=8,'y'=4] {'c'}, dimensions={0} | all-to-all | bytes 5767168 | tf_op jit(solution)/shard_map/all_to_all | solution.py:219
  79.9 2.1 %reduce_sum.30 = bf16[512,1408]{1,0:T(8,128)(2,1)} reduce(bf16[2,512,1408]{2,1,0:T(8,128)(2,1)S(1)} %all_to_all.42, bf16[]{:T(256)} %constant.6.clone.1), dimensions={0}, to_apply=%region_0.0 | reduce | flops 720896 | bytes 4325378 | tf_op jit(solution)/shard_map/reduce_sum | solution.py:232
  82.0 23.4 %all_to_all.43 = bf16[16,32,1408]{2,1,0:T(8,128)(2,1)S(1)} all-to-all(bf16[16,32,1408]{2,1,0:T(8,128)(2,1)} %bitcast.17), channel_id=1, replica_groups=mesh['x'=4,'c'=2,'z'=8,'y'=4] {'x','y'}, dimensions={0} | all-to-all | bytes 2883584 | tf_op jit(solution)/shard_map/all_to_all | solution.py:219
  105.4 0.9 convert_reduce_fusion.part_ref
  106.3 1.6 %pack.1 = bf16[8,16,1024]{2,1,0:T(8,128)(2,1)} custom-call(f32[32,1408]{1,0:T(8,128)} %convert_reduce_fusion.part_ref), custom_call_target="tpu_custom_call" | custom-call | tf_op jit(solution)/shard_map/pack/pallas_call | solution.py:144
  107.9 8.2 %all-to-all-start.4 = ((bf16[8,16,1024]{2,1,0:T(8,128)(2,1)}), bf16[8,16,1024]{2,1,0:T(8,128)(2,1)S(1)}, u32[]{:S(2)}, u32[]{:S(2)}) async-start(bf16[8,16,1024]{2,1,0:T(8,128)(2,1)} %pack.1), calls=%async_computation.4 | async-start | bytes 524288 | tf_op jit(solution)/shard_map/all_to_all | solution.py:219
  116.1 9.4 %all-to-all-done.4 = bf16[8,16,1024]{2,1,0:T(8,128)(2,1)S(1)} async-done(((bf16[8,16,1024]{2,1,0:T(8,128)(2,1)}), bf16[8,16,1024]{2,1,0:T(8,128)(2,1)S(1)}, u32[]{:S(2)}, u32[]{:S(2)}) %all-to-all-start.4) | async-done | bytes 262176 | tf_op jit(solution)/shard_map/all_to_all | solution.py:219
  125.6 0.8 fusion
  126.4 0.8 broadcast_in_dim.6
  127.2 4.3 %all-to-all-start.5 = ((f32[16,32,256]{2,1,0:T(8,128)}), f32[16,32,256]{2,1,0:T(8,128)S(1)}, u32[]{:S(2)}, u32[]{:S(2)}) async-start(f32[16,32,256]{2,1,0:T(8,128)} %broadcast_in_dim.6), calls=%async_computation.5 | async-start | bytes 1048576 | tf_op jit(solution)/shard_map/all_to_all | solution.py:219
  131.5 0.6 slice_multiply_fusion
  132.1 8.3 %all-to-all-done.5 = f32[16,32,256]{2,1,0:T(8,128)S(1)} async-done(((f32[16,32,256]{2,1,0:T(8,128)}), f32[16,32,256]{2,1,0:T(8,128)S(1)}, u32[]{:S(2)}, u32[]{:S(2)}) %all-to-all-start.5) | async-done | bytes 524320 | tf_op jit(solution)/shard_map/all_to_all | solution.py:219
  140.5 0.1 broadcast_in_dim.7
  140.5 9.0 %all_to_all.44 = f32[2,512,256]{2,1,0:T(8,128)S(1)} all-to-all(f32[2,512,256]{2,1,0:T(8,128)S(1)} %broadcast_in_dim.7), channel_id=1, replica_groups=mesh['x'=4,'c'=2,'z'=8,'y'=4] {'c'}, dimensions={0} | all-to-all | bytes 2097152 | tf_op jit(solution)/shard_map/all_to_all | solution.py:219
  149.5 1.0 copy.11
  (3 shorter events, 0.1 us)
Async XLA Ops:
  20.7 30.4 %all-to-all-start.1 = ((bf16[8,128,1024]{2,1,0:T(8,128)(2,1)}), bf16[8,128,1024]{2,1,0:T(8,128)(2,1)S(1)}, u32[]{:S(2)}, u32[]{:S(2)}) async-start(bf16[8,128,1024]{2,1,0:T(8,128)(2,1)} %bitcast.15), calls=%async_computation.1 | async-start | bytes 4194304 | tf_op jit(solution)/shard_map/all_to_all | solution.py:219
  51.1 1.4 copy-start
  107.9 17.6 %all-to-all-start.4 = ((bf16[8,16,1024]{2,1,0:T(8,128)(2,1)}), bf16[8,16,1024]{2,1,0:T(8,128)(2,1)S(1)}, u32[]{:S(2)}, u32[]{:S(2)}) async-start(bf16[8,16,1024]{2,1,0:T(8,128)(2,1)} %pack.1), calls=%async_computation.4 | async-start | bytes 524288 | tf_op jit(solution)/shard_map/all_to_all | solution.py:219
  127.2 13.3 %all-to-all-start.5 = ((f32[16,32,256]{2,1,0:T(8,128)}), f32[16,32,256]{2,1,0:T(8,128)S(1)}, u32[]{:S(2)}, u32[]{:S(2)}) async-start(f32[16,32,256]{2,1,0:T(8,128)} %broadcast_in_dim.6), calls=%async_computation.5 | async-start | bytes 1048576 | tf_op jit(solution)/shard_map/all_to_all | solution.py:219

commit v6 on v5

--- a/solution.py
+++ b/solution.py
@@ -219,6 +219,10 @@
     return lax.all_to_all(value, axis, split_axis=0, concat_axis=0, tiled=True)
 
 
+def with_pair(value):
+    return lax.ppermute(value, "c", [(0, 1), (1, 0)])
+
+
 def sent_to_all(value, axis):
     copies = jnp.broadcast_to(value, (lax.axis_size(axis), *value.shape))
     return swap(copies, axis).reshape(-1, value.shape[-1])
@@ -229,7 +233,11 @@
     centres = find_centres(swap(ids, GRP), centroids)
     got = swap(centres, GRP).reshape(OWNERS * CAP, D)
     part = code_stats(tokens, slot, got, rotation, split_codes(codebook))
-    part = swap(part.reshape(2, 512, WIDE), "c").astype(F32).sum(axis=0).astype(BF16)
+    core = lax.axis_index("c")
+    halves = part.reshape(2, 512, WIDE)
+    mine = lax.dynamic_index_in_dim(halves, core, 0, keepdims=False)
+    other = lax.dynamic_index_in_dim(halves, 1 - core, 0, keepdims=False)
+    part = (mine.astype(F32) + with_pair(other).astype(F32)).astype(BF16)
     part = swap(part.reshape(16, 32, WIDE), XY).astype(F32).sum(axis=0)
     part = swap(pack(part), "z").astype(F32).sum(axis=0)
     cross_cov = part[:4] * (1.0 / math.sqrt(ROWS * 256))
@@ -237,7 +245,9 @@
     book = lax.dynamic_slice_in_dim(codebook.reshape(M * DSUB, K), place * 32, 32, 0)
     num = jnp.concatenate([part[8:, b * K : (b + 1) * K] for b in range(4)], axis=0)
     fresh = (num + book) / (part[4:5, :K] + part[5:6, :K] + 1.0)
-    fresh = sent_to_all(sent_to_all(fresh, XY), "c")
+    fresh = sent_to_all(fresh, XY)
+    other = with_pair(fresh)
+    fresh = jnp.where(core == 0, jnp.stack([fresh, other]), jnp.stack([other, fresh]))
     return (fresh.reshape(M, DSUB, K), cross_cov)
 
 

time: 151 us -> 146 us (0.967)
  waiting for transfers between devices: 40.3 us -> 36.1 us
  blocking collectives: 51.8 us -> 47.8 us
    all_to_all x3 -> x2, waiting for transfers between devices: 40.3 us -> 32 us  [swap(): return lax.all_to_all(value, axis, split_axis=0, concat_axis=0, tiled=True)]
    ppermute x0 -> x2, starting transfers between devices: none -> 5.65 us  [with_pair(): return lax.ppermute(value, 'c', [(0, 1), (1, 0)])]
    all_to_all x3 -> x2, starting transfers between devices: 16.5 us -> 12.2 us  [swap(): return lax.all_to_all(value, axis, split_axis=0, concat_axis=0, tiled=True)]
    ppermute x0 -> x2, waiting for transfers between devices: none -> 4.12 us  [with_pair(): return lax.ppermute(value, 'c', [(0, 1), (1, 0)])]
    all_to_all x4 -> x3, blocking collectives: 51.8 us -> 47.8 us  [swap(): return lax.all_to_all(value, axis, split_axis=0, concat_axis=0, tiled=True)]
    squeeze x0 -> x1, local copies, waits for them, and re-layouts: none -> 2.76 us  [local(): other = lax.dynamic_index_in_dim(halves, 1 - core, 0, keepdims=False)]
    reduce_sum x1 -> x0, other arithmetic: 2.05 us -> none  [local(): swap(part.reshape(2, 512, WIDE), 'c').astype(F32).sum(axis=0).astype(BF16)]
    convert_element_type x0 -> x1, other arithmetic: none -> 1.7 us  [local(): part = (mine.astype(F32) + with_pair(other).astype(F32)).astype(BF16)]
  transfers between devices with their start and end apart: 3 -> 4, of which waited for: 3 -> 4; matrix products, arithmetic and copies ran while one was open for 0% -> 0% of each run, Pallas kernels for 3% -> 3%
where the time goes in v6:
time: 146 us; the launch traced here: 145 us
  blocking collectives  47.8 us (33%)
  waiting for transfers between devices  36.1 us (25%)
  Pallas kernels  33.6 us (23%)
  starting transfers between devices  17.9 us (12%)
  other arithmetic  5.03 us (3%)
  local copies, waits for them, and re-layouts  4.17 us (3%)
    all_to_all x3, blocking collectives, swap(): return lax.all_to_all(value, axis, split_axis=0, concat_axis=0, tiled=True)  47.8 us
    all_to_all x2, waiting for transfers between devices, swap(): return lax.all_to_all(value, axis, split_axis=0, concat_axis=0, tiled=True)  32 us
    pallas_call x1, Pallas kernels, code_stats(): pl.pallas_call(stats_kernel, grid=(M // 4,), in_specs=[whole((ROWS, D)),...  19.7 us
    all_to_all x2, starting transfers between devices, swap(): return lax.all_to_all(value, axis, split_axis=0, concat_axis=0, tiled=True)  12.2 us
    pallas_call x1, Pallas kernels, find_centres(): pl.pallas_call(centres_kernel, grid=(D // 256,), in_specs=[whole((OWNERS,...  5.79 us
    ppermute x2, starting transfers between devices, with_pair(): return lax.ppermute(value, 'c', [(0, 1), (1, 0)])  5.65 us
    ppermute x2, waiting for transfers between devices, with_pair(): return lax.ppermute(value, 'c', [(0, 1), (1, 0)])  4.12 us
    pallas_call x1, Pallas kernels, split_codes(): pl.pallas_call(codes_kernel, grid=(M // 4,), in_specs=[block(DSUB, K)], o...  3.79 us
  transfers between devices with their start and end apart: 4, of which 4 were waited for; matrix products, arithmetic and copies ran while one was open for 0% of the time, Pallas kernels for 3%

profile of v6, /device:TPU:1, one launch (start us, length us, event | category | flops | bytes accessed | tf_op | source)
XLA Modules:
  0.0 145.3 jit_solution(397326670288360657)
XLA Ops:
  0.6 2.7 %slots.1 = (s32[512,1]{1,0:T(8,128)}, s32[8,128]{1,0:T(8,128)}) custom-call(s32[1,512]{1,0:T(1,128)} %bitcast.34, s32[1,512]{1,0:T(1,128)} %bitcast.35), custom_call_target="tpu_custom_call" | custom-call | tf_op jit(solution)/shard_map/slots/pallas_call | solution.py:154
  3.3 11.6 %all_to_all.31 = s32[8,1,128]{2,1,0:T(1,128)} all-to-all(s32[8,1,128]{2,1,0:T(1,128)} %bitcast.33), channel_id=1, replica_groups=mesh['x'=4,'c'=2,'z'=8,'y'=4] {'x','c'}, dimensions={0} | all-to-all | bytes 8192 | tf_op jit(solution)/shard_map/all_to_all | solution.py:219
  14.8 5.8 %centres.1 = bf16[1024,1024]{1,0:T(8,128)(2,1)} custom-call(s32[8,128]{1,0:T(8,128)} %bitcast.31, bf16[1024,1024]{1,0:T(8,128)(2,1)} %centroids_ref.1), custom_call_target="tpu_custom_call" | custom-call | tf_op jit(solution)/shard_map/centres/pallas_call | solution.py:166
  20.6 4.0 %all-to-all-start.1 = ((bf16[8,128,1024]{2,1,0:T(8,128)(2,1)}), bf16[8,128,1024]{2,1,0:T(8,128)(2,1)S(1)}, u32[]{:S(2)}, u32[]{:S(2)}) async-start(bf16[8,128,1024]{2,1,0:T(8,128)(2,1)} %bitcast.23), calls=%async_computation.1 | async-start | bytes 4194304 | tf_op jit(solution)/shard_map/all_to_all | solution.py:219
  24.7 3.8 %codes.1 = (bf16[16,256,256]{2,1,0:T(8,128)(2,1)}, bf16[16,256,128]{2,1,0:T(8,128)(2,1)}, f32[16,1,256]{2,1,0:T(1,128)}) custom-call(f32[16,64,256]{2,1,0:T(8,128)} %book_ref.1), custom_call_target="tpu_custom_call" | custom-call | tf_op jit(solution)/shard_map/codes/pallas_call | solution.py:181
  28.5 22.6 %all-to-all-done.1 = bf16[8,128,1024]{2,1,0:T(8,128)(2,1)S(1)} async-done(((bf16[8,128,1024]{2,1,0:T(8,128)(2,1)}), bf16[8,128,1024]{2,1,0:T(8,128)(2,1)S(1)}, u32[]{:S(2)}, u32[]{:S(2)}) %all-to-all-start.1) | async-done | bytes 2097184 | tf_op jit(solution)/shard_map/all_to_all | solution.py:219
  51.0 0.0 copy-start.1
  51.0 1.4 copy-done.1
  52.4 19.7 %stats.1 = bf16[1024,1408]{1,0:T(8,128)(2,1)} custom-call(bf16[512,1024]{1,0:T(8,128)(2,1)} %tokens_ref.1, s32[512,1]{1,0:T(8,128)} %get-tuple-element.7.slot_ref, bf16[1024,1024]{1,0:T(8,128)(2,1)} %bitcast.24, bf16[1024,1024]{1,0:T(8,128)(2,1)} %rotation_ref.1, bf16[16,256,256]{2,1,0:T(8,128)(2,1)} %get-tuple-element.9.stack_ref, ...), custom_call_target="tpu_custom_call" | custom-call | tf_op jit(solution)/shard_map/stats/pallas_call | solution.py:199
  72.1 0.0 copy-start
  72.1 2.8 %dynamic-slice_bitcast_fusion = bf16[512,1408]{1,0:T(8,128)(2,1)} fusion(bf16[2,512,1408]{2,1,0:T(8,128)(2,1)} %bitcast.21, s32[]{:T(128)S(6)} %select_n.24), kind=kLoop, calls=%fused_computation.3 | loop fusion | bytes 2883588 | tf_op jit(solution)/shard_map/jit(dynamic_index_in_dim)/squeeze | solution.py:239
  74.9 0.9 collective-permute-start
  75.7 3.2 %collective-permute-done = bf16[512,1408]{1,0:T(8,128)(2,1)} collective-permute-done((bf16[512,1408]{1,0:T(8,128)(2,1)}, bf16[512,1408]{1,0:T(8,128)(2,1)}, u32[]{:S(2)}, u32[]{:S(2)}) %collective-permute-start) | collective-permute-done | bytes 1441824 | tf_op jit(solution)/shard_map/ppermute | solution.py:223
  78.9 0.0 copy-done
  78.9 1.7 %fusion = bf16[512,1408]{1,0:T(8,128)(2,1)S(1)} fusion(bf16[512,1408]{1,0:T(8,128)(2,1)} %collective-permute-done, bf16[2,512,1408]{2,1,0:T(8,128)(2,1)S(1)} %bitcast.22, s32[]{:T(128)S(6)} %select_n.23), kind=kLoop, calls=%fused_computation.1 | loop fusion | flops 2883584 | bytes 4325380 | tf_op jit(solution)/shard_map/convert_element_type | solution.py:240
  80.6 23.2 %all_to_all.32 = bf16[16,32,1408]{2,1,0:T(8,128)(2,1)S(1)} all-to-all(bf16[16,32,1408]{2,1,0:T(8,128)(2,1)S(1)} %bitcast.25), channel_id=1, replica_groups=mesh['x'=4,'c'=2,'z'=8,'y'=4] {'x','y'}, dimensions={0} | all-to-all | bytes 2883584 | tf_op jit(solution)/shard_map/all_to_all | solution.py:219
  103.9 0.9 convert_reduce_fusion.part_ref
  104.7 1.6 %pack.1 = bf16[8,16,1024]{2,1,0:T(8,128)(2,1)} custom-call(f32[32,1408]{1,0:T(8,128)} %convert_reduce_fusion.part_ref), custom_call_target="tpu_custom_call" | custom-call | tf_op jit(solution)/shard_map/pack/pallas_call | solution.py:144
  106.4 8.2 %all-to-all-start.3 = ((bf16[8,16,1024]{2,1,0:T(8,128)(2,1)}), bf16[8,16,1024]{2,1,0:T(8,128)(2,1)S(1)}, u32[]{:S(2)}, u32[]{:S(2)}) async-start(bf16[8,16,1024]{2,1,0:T(8,128)(2,1)} %pack.1), calls=%async_computation.3 | async-start | bytes 524288 | tf_op jit(solution)/shard_map/all_to_all | solution.py:219
  114.6 9.4 %all-to-all-done.3 = bf16[8,16,1024]{2,1,0:T(8,128)(2,1)S(1)} async-done(((bf16[8,16,1024]{2,1,0:T(8,128)(2,1)}), bf16[8,16,1024]{2,1,0:T(8,128)(2,1)S(1)}, u32[]{:S(2)}, u32[]{:S(2)}) %all-to-all-start.3) | async-done | bytes 262176 | tf_op jit(solution)/shard_map/all_to_all | solution.py:219
  124.0 0.8 fusion.1
  124.9 13.0 %all_to_all.33 = f32[16,32,256]{2,1,0:T(8,128)S(1)} all-to-all(f32[16,32,256]{2,1,0:T(8,128)S(1)} %broadcast_in_dim.3), channel_id=1, replica_groups=mesh['x'=4,'c'=2,'z'=8,'y'=4] {'x','y'}, dimensions={0} | all-to-all | bytes 1048576 | tf_op jit(solution)/shard_map/all_to_all | solution.py:219
  137.9 4.8 %collective-permute-start.1 = (f32[512,256]{1,0:T(8,128)S(1)}, f32[512,256]{1,0:T(8,128)S(1)}, u32[]{:S(2)}, u32[]{:S(2)}) collective-permute-start(f32[512,256]{1,0:T(8,128)S(1)} %bitcast.26), channel_id=1, source_target_pairs={{0,32},{32,0},{1,33},{33,1},{2,34},{34,2},{3,35},{35,3},{4,36},{36... | collective-permute-start | bytes 1572872 | tf_op jit(solution)/shard_map/ppermute | solution.py:223
  142.7 0.6 slice_multiply_fusion
  143.3 0.9 collective-permute-done.1
  144.2 1.0 maximum_select_fusion
  (4 shorter events, 0.1 us)
Async XLA Ops:
  20.6 30.4 %all-to-all-start.1 = ((bf16[8,128,1024]{2,1,0:T(8,128)(2,1)}), bf16[8,128,1024]{2,1,0:T(8,128)(2,1)S(1)}, u32[]{:S(2)}, u32[]{:S(2)}) async-start(bf16[8,128,1024]{2,1,0:T(8,128)(2,1)} %bitcast.23), calls=%async_computation.1 | async-start | bytes 4194304 | tf_op jit(solution)/shard_map/all_to_all | solution.py:219
  51.0 1.4 copy-start.1
  72.1 6.8 %copy-start = (bf16[1024,1408]{1,0:T(8,128)(2,1)S(1)}, bf16[1024,1408]{1,0:T(8,128)(2,1)}, u32[]{:S(2)}) copy-start(bf16[1024,1408]{1,0:T(8,128)(2,1)} %stats.1) | copy-start | bytes 8650756
  74.9 4.1 %collective-permute-start = (bf16[512,1408]{1,0:T(8,128)(2,1)}, bf16[512,1408]{1,0:T(8,128)(2,1)}, u32[]{:S(2)}, u32[]{:S(2)}) collective-permute-start(bf16[512,1408]{1,0:T(8,128)(2,1)} %dynamic-slice_bitcast_fusion), channel_id=1, source_target_pairs={{0,32},{32,0},{1,33},{33,1},{2,34},{34,2},{3,35},{35,3},{4,36},{36... | collective-permute-start | bytes 4325384 | tf_op jit(solution)/shard_map/ppermute | solution.py:223
  106.4 17.6 %all-to-all-start.3 = ((bf16[8,16,1024]{2,1,0:T(8,128)(2,1)}), bf16[8,16,1024]{2,1,0:T(8,128)(2,1)S(1)}, u32[]{:S(2)}, u32[]{:S(2)}) async-start(bf16[8,16,1024]{2,1,0:T(8,128)(2,1)} %pack.1), calls=%async_computation.3 | async-start | bytes 524288 | tf_op jit(solution)/shard_map/all_to_all | solution.py:219
  137.9 6.3 %collective-permute-start.1 = (f32[512,256]{1,0:T(8,128)S(1)}, f32[512,256]{1,0:T(8,128)S(1)}, u32[]{:S(2)}, u32[]{:S(2)}) collective-permute-start(f32[512,256]{1,0:T(8,128)S(1)} %bitcast.26), channel_id=1, source_target_pairs={{0,32},{32,0},{1,33},{33,1},{2,34},{34,2},{3,35},{35,3},{4,36},{36... | collective-permute-start | bytes 1572872 | tf_op jit(solution)/shard_map/ppermute | solution.py:223

commit v7 on v6

--- a/solution.py
+++ b/solution.py
@@ -77,7 +77,7 @@
 
 
 def stats_kernel(
-    tokens_ref, slot_ref, got_ref, rotation_ref, stack_ref, turned_ref, norm_ref,
+    core_ref, tokens_ref, slot_ref, got_ref, rotation_ref, stack_ref, turned_ref, norm_ref,
     out_ref, res_ref, turned_res_ref,
 ):
     step = pl.program_id(0)
@@ -90,7 +90,7 @@
         res_ref[...] = res
         d = iota((D, D), 1)
         place = (
-            ((d >> 7) & 1) * 512 + (d >> 8) * 128 + ((d >> 2) & 3) * 32 + ((d >> 4) & 7) * 4
+            (((d >> 7) & 1) ^ core_ref[0]) * 512 + (d >> 8) * 128 + ((d >> 2) & 3) * 32 + ((d >> 4) & 7) * 4
         ) + (d & 3)
         turned_res_ref[...] = dot(one_hot(iota((D, D), 0) == place), res, 1, 1).astype(BF16)
 
@@ -114,7 +114,7 @@
             prob = prob.astype(BF16)
             split = jnp.where(left, high.astype(F32), rest).astype(BF16)
             num = dot(split, prob, 0, 0)
-            at = pl.ds(pl.multiple_of(step * 256 + m * DSUB, DSUB), DSUB)
+            at = pl.ds(pl.multiple_of((step * 256 + m * DSUB + core_ref[0] * 512) & (D - 1), DSUB), DSUB)
             out_ref[at, D : D + K] = (num[:DSUB] + num[DSUB:]).astype(BF16)
             row = iota((DSUB, 128), 0) % 32
             masses = jnp.where(row == 0, mass[:, :128], jnp.where(row == 1, mass[:, 128:], 0.0))
@@ -192,7 +192,7 @@
     )(codebook)
 
 
-def code_stats(tokens, slot, got, rotation, codes):
+def code_stats(core, tokens, slot, got, rotation, codes):
     def block(*shape):
         return pl.BlockSpec((4, *shape), lambda i: (i, 0, 0))
 
@@ -200,6 +200,7 @@
         stats_kernel,
         grid=(M // 4,),
         in_specs=[
+            pl.BlockSpec(memory_space=pltpu.SMEM),
             whole((ROWS, D)),
             whole((ROWS, 1)),
             whole((OWNERS * CAP, D)),
@@ -212,7 +213,7 @@
         out_shape=jax.ShapeDtypeStruct((D, WIDE), BF16),
         scratch_shapes=[pltpu.VMEM((ROWS, D), BF16), pltpu.VMEM((D, ROWS), BF16)],
         name="stats",
-    )(tokens, slot, got, rotation, *codes)
+    )(core.reshape(1), tokens, slot, got, rotation, *codes)
 
 
 def swap(value, axis):
@@ -232,11 +233,9 @@
     slot, ids = find_slots(owner, list_local)
     centres = find_centres(swap(ids, GRP), centroids)
     got = swap(centres, GRP).reshape(OWNERS * CAP, D)
-    part = code_stats(tokens, slot, got, rotation, split_codes(codebook))
     core = lax.axis_index("c")
-    halves = part.reshape(2, 512, WIDE)
-    mine = lax.dynamic_index_in_dim(halves, core, 0, keepdims=False)
-    other = lax.dynamic_index_in_dim(halves, 1 - core, 0, keepdims=False)
+    part = code_stats(core, tokens, slot, got, rotation, split_codes(codebook))
+    mine, other = part[:512], part[512:]
     part = (mine.astype(F32) + with_pair(other).astype(F32)).astype(BF16)
     part = swap(part.reshape(16, 32, WIDE), XY).astype(F32).sum(axis=0)
     part = swap(pack(part), "z").astype(F32).sum(axis=0)

time: 146 us -> 143 us (0.979)
    squeeze x1 -> x0, local copies, waits for them, and re-layouts: 2.76 us -> none  [local(): other = lax.dynamic_index_in_dim(halves, 1 - core, 0, keepdims=False)]
    slice x0 -> x1, local copies, waits for them, and re-layouts: none -> 1.62 us  [local(): mine, other = (part[:512], part[512:])]
where the time goes in v7:
time: 143 us
  blocking collectives  47.8 us (33%)
  waiting for transfers between devices  35.7 us (25%)
  Pallas kernels  33.6 us (23%)
  starting transfers between devices  18 us (13%)
  other arithmetic  3.68 us (3%)
  local copies, waits for them, and re-layouts  3.03 us (2%)
    all_to_all x3, blocking collectives, swap(): return lax.all_to_all(value, axis, split_axis=0, concat_axis=0, tiled=True)  47.8 us
    all_to_all x2, waiting for transfers between devices, swap(): return lax.all_to_all(value, axis, split_axis=0, concat_axis=0, tiled=True)  32 us
    pallas_call x1, Pallas kernels, code_stats(): pl.pallas_call(stats_kernel, grid=(M // 4,), in_specs=[pl.BlockSpec(memor...  19.7 us
    all_to_all x2, starting transfers between devices, swap(): return lax.all_to_all(value, axis, split_axis=0, concat_axis=0, tiled=True)  12.2 us
    pallas_call x1, Pallas kernels, find_centres(): pl.pallas_call(centres_kernel, grid=(D // 256,), in_specs=[whole((OWNERS,...  5.79 us
    ppermute x2, starting transfers between devices, with_pair(): return lax.ppermute(value, 'c', [(0, 1), (1, 0)])  5.74 us
    pallas_call x1, Pallas kernels, split_codes(): pl.pallas_call(codes_kernel, grid=(M // 4,), in_specs=[block(DSUB, K)], o...  3.79 us
    ppermute x2, waiting for transfers between devices, with_pair(): return lax.ppermute(value, 'c', [(0, 1), (1, 0)])  3.78 us
  transfers between devices with their start and end apart: 4, of which 4 were waited for; matrix products, arithmetic and copies ran while one was open for 0% of the time, Pallas kernels for 3%

profile of v7, /device:TPU:1, one launch (start us, length us, event | category | flops | bytes accessed | tf_op | source)
XLA Modules:
  0.0 142.5 jit_solution(9627595181885257463)
XLA Ops:
  0.6 2.7 %slots.1 = (s32[512,1]{1,0:T(8,128)}, s32[8,128]{1,0:T(8,128)}) custom-call(s32[1,512]{1,0:T(1,128)} %bitcast.27, s32[1,512]{1,0:T(1,128)} %bitcast.28), custom_call_target="tpu_custom_call" | custom-call | tf_op jit(solution)/shard_map/slots/pallas_call | solution.py:154
  3.3 11.6 %all_to_all.31 = s32[8,1,128]{2,1,0:T(1,128)} all-to-all(s32[8,1,128]{2,1,0:T(1,128)} %bitcast.26), channel_id=1, replica_groups=mesh['x'=4,'c'=2,'z'=8,'y'=4] {'x','c'}, dimensions={0} | all-to-all | bytes 8192 | tf_op jit(solution)/shard_map/all_to_all | solution.py:220
  14.8 5.8 %centres.1 = bf16[1024,1024]{1,0:T(8,128)(2,1)} custom-call(s32[8,128]{1,0:T(8,128)} %bitcast.24, bf16[1024,1024]{1,0:T(8,128)(2,1)} %centroids_ref.1), custom_call_target="tpu_custom_call" | custom-call | tf_op jit(solution)/shard_map/centres/pallas_call | solution.py:166
  20.6 4.0 %all-to-all-start.1 = ((bf16[8,128,1024]{2,1,0:T(8,128)(2,1)}), bf16[8,128,1024]{2,1,0:T(8,128)(2,1)S(1)}, u32[]{:S(2)}, u32[]{:S(2)}) async-start(bf16[8,128,1024]{2,1,0:T(8,128)(2,1)} %bitcast.16), calls=%async_computation.1 | async-start | bytes 4194304 | tf_op jit(solution)/shard_map/all_to_all | solution.py:220
  24.7 3.8 %codes.1 = (bf16[16,256,256]{2,1,0:T(8,128)(2,1)}, bf16[16,256,128]{2,1,0:T(8,128)(2,1)}, f32[16,1,256]{2,1,0:T(1,128)}) custom-call(f32[16,64,256]{2,1,0:T(8,128)} %book_ref.1), custom_call_target="tpu_custom_call" | custom-call | tf_op jit(solution)/shard_map/codes/pallas_call | solution.py:181
  28.5 22.6 %all-to-all-done.1 = bf16[8,128,1024]{2,1,0:T(8,128)(2,1)S(1)} async-done(((bf16[8,128,1024]{2,1,0:T(8,128)(2,1)}), bf16[8,128,1024]{2,1,0:T(8,128)(2,1)S(1)}, u32[]{:S(2)}, u32[]{:S(2)}) %all-to-all-start.1) | async-done | bytes 2097184 | tf_op jit(solution)/shard_map/all_to_all | solution.py:220
  51.0 0.0 copy-start.1
  51.0 1.4 copy-done.1
  52.4 19.7 %stats.1 = bf16[1024,1408]{1,0:T(8,128)(2,1)} custom-call(s32[1]{0:T(128)} %bitcast.core_ref, bf16[512,1024]{1,0:T(8,128)(2,1)} %tokens_ref.1, s32[512,1]{1,0:T(8,128)} %get-tuple-element.7.slot_ref, bf16[1024,1024]{1,0:T(8,128)(2,1)} %bitcast.17, bf16[1024,1024]{1,0:T(8,128)(2,1)} %rotation_ref.1, bf16[16,256,256]{2,1,0:T(8,128)(2,1)} %get-tuple-element.9.stack_ref, ...), custom_call_target="tpu_custom_call" | custom-call | tf_op jit(solution)/shard_map/stats/pallas_call | solution.py:199
  72.1 0.0 copy-start
  72.1 1.6 %slice.37 = bf16[512,1408]{1,0:T(8,128)(2,1)S(1)} slice(bf16[1024,1408]{1,0:T(8,128)(2,1)} %stats.1), slice={[512:1024], [0:1408]} | slice | bytes 2883584 | tf_op jit(solution)/shard_map/slice | solution.py:238
  73.7 1.0 collective-permute-start
  74.7 2.8 %collective-permute-done = bf16[512,1408]{1,0:T(8,128)(2,1)S(1)} collective-permute-done((bf16[512,1408]{1,0:T(8,128)(2,1)S(1)}, bf16[512,1408]{1,0:T(8,128)(2,1)S(1)}, u32[]{:S(2)}, u32[]{:S(2)}) %collective-permute-start) | collective-permute-done | bytes 1441824 | tf_op jit(solution)/shard_map/ppermute | solution.py:224
  77.5 0.0 copy-done
  77.5 0.3 add_convert_fusion
  77.9 23.2 %all_to_all.32 = bf16[16,32,1408]{2,1,0:T(8,128)(2,1)S(1)} all-to-all(bf16[16,32,1408]{2,1,0:T(8,128)(2,1)S(1)} %bitcast.18), channel_id=1, replica_groups=mesh['x'=4,'c'=2,'z'=8,'y'=4] {'x','y'}, dimensions={0} | all-to-all | bytes 2883584 | tf_op jit(solution)/shard_map/all_to_all | solution.py:220
  101.1 0.9 convert_reduce_fusion.part_ref
  102.0 1.6 %pack.1 = bf16[8,16,1024]{2,1,0:T(8,128)(2,1)} custom-call(f32[32,1408]{1,0:T(8,128)} %convert_reduce_fusion.part_ref), custom_call_target="tpu_custom_call" | custom-call | tf_op jit(solution)/shard_map/pack/pallas_call | solution.py:144
  103.6 8.2 %all-to-all-start.3 = ((bf16[8,16,1024]{2,1,0:T(8,128)(2,1)}), bf16[8,16,1024]{2,1,0:T(8,128)(2,1)S(1)}, u32[]{:S(2)}, u32[]{:S(2)}) async-start(bf16[8,16,1024]{2,1,0:T(8,128)(2,1)} %pack.1), calls=%async_computation.3 | async-start | bytes 524288 | tf_op jit(solution)/shard_map/all_to_all | solution.py:220
  111.8 9.4 %all-to-all-done.3 = bf16[8,16,1024]{2,1,0:T(8,128)(2,1)S(1)} async-done(((bf16[8,16,1024]{2,1,0:T(8,128)(2,1)}), bf16[8,16,1024]{2,1,0:T(8,128)(2,1)S(1)}, u32[]{:S(2)}, u32[]{:S(2)}) %all-to-all-start.3) | async-done | bytes 262176 | tf_op jit(solution)/shard_map/all_to_all | solution.py:220
  121.3 0.8 fusion
  122.1 13.0 %all_to_all.33 = f32[16,32,256]{2,1,0:T(8,128)S(1)} all-to-all(f32[16,32,256]{2,1,0:T(8,128)S(1)} %broadcast_in_dim.3), channel_id=1, replica_groups=mesh['x'=4,'c'=2,'z'=8,'y'=4] {'x','y'}, dimensions={0} | all-to-all | bytes 1048576 | tf_op jit(solution)/shard_map/all_to_all | solution.py:220
  135.2 4.8 %collective-permute-start.1 = (f32[512,256]{1,0:T(8,128)S(1)}, f32[512,256]{1,0:T(8,128)S(1)}, u32[]{:S(2)}, u32[]{:S(2)}) collective-permute-start(f32[512,256]{1,0:T(8,128)S(1)} %bitcast.19), channel_id=1, source_target_pairs={{0,32},{32,0},{1,33},{33,1},{2,34},{34,2},{3,35},{35,3},{4,36},{36... | collective-permute-start | bytes 1572872 | tf_op jit(solution)/shard_map/ppermute | solution.py:224
  140.0 0.6 slice_multiply_fusion
  140.6 0.9 collective-permute-done.1
  141.5 1.0 maximum_select_fusion
  (4 shorter events, 0.1 us)
Async XLA Ops:
  20.6 30.4 %all-to-all-start.1 = ((bf16[8,128,1024]{2,1,0:T(8,128)(2,1)}), bf16[8,128,1024]{2,1,0:T(8,128)(2,1)S(1)}, u32[]{:S(2)}, u32[]{:S(2)}) async-start(bf16[8,128,1024]{2,1,0:T(8,128)(2,1)} %bitcast.16), calls=%async_computation.1 | async-start | bytes 4194304 | tf_op jit(solution)/shard_map/all_to_all | solution.py:220
  51.0 1.4 copy-start.1
  72.1 5.4 %copy-start = (bf16[1024,1408]{1,0:T(8,128)(2,1)S(1)}, bf16[1024,1408]{1,0:T(8,128)(2,1)}, u32[]{:S(2)}) copy-start(bf16[1024,1408]{1,0:T(8,128)(2,1)} %stats.1) | copy-start | bytes 8650756
  73.7 3.8 %collective-permute-start = (bf16[512,1408]{1,0:T(8,128)(2,1)S(1)}, bf16[512,1408]{1,0:T(8,128)(2,1)S(1)}, u32[]{:S(2)}, u32[]{:S(2)}) collective-permute-start(bf16[512,1408]{1,0:T(8,128)(2,1)S(1)} %slice.37), channel_id=1, source_target_pairs={{0,32},{32,0},{1,33},{33,1},{2,34},{34,2},{3,35},{35,3},{4,36},{36... | collective-permute-start | bytes 4325384 | tf_op jit(solution)/shard_map/ppermute | solution.py:224
  103.6 17.6 %all-to-all-start.3 = ((bf16[8,16,1024]{2,1,0:T(8,128)(2,1)}), bf16[8,16,1024]{2,1,0:T(8,128)(2,1)S(1)}, u32[]{:S(2)}, u32[]{:S(2)}) async-start(bf16[8,16,1024]{2,1,0:T(8,128)(2,1)} %pack.1), calls=%async_computation.3 | async-start | bytes 524288 | tf_op jit(solution)/shard_map/all_to_all | solution.py:220
  135.2 6.3 %collective-permute-start.1 = (f32[512,256]{1,0:T(8,128)S(1)}, f32[512,256]{1,0:T(8,128)S(1)}, u32[]{:S(2)}, u32[]{:S(2)}) collective-permute-start(f32[512,256]{1,0:T(8,128)S(1)} %bitcast.19), channel_id=1, source_target_pairs={{0,32},{32,0},{1,33},{33,1},{2,34},{34,2},{3,35},{35,3},{4,36},{36... | collective-permute-start | bytes 1572872 | tf_op jit(solution)/shard_map/ppermute | solution.py:224
